TPU v7x, 32 devices: a whole 2x2x4 slice. The times are simulated.
32 devices in a mesh: slab: 16 (over z, y, core), head: 2 (over x).
Axes of the slice: x: 2, y: 2, z: 4, core: 2. Of those that a mesh axis runs over, the one named last changes fastest.
Arguments:
- queries: bfloat16 [8192, 1024], P('slab', 'head'), may hold values from -6.5 to 6.5
- key_values: bfloat16 [8192, 4096], P('slab', 'head'), may hold values from -6.5 to 6.5
- out_grads: bfloat16 [8192, 2560], P('slab', 'head'), may hold values from -6 to 6
- positions: float32 [3, 8192], P(None, 'slab'), may hold values from 0 to 4, as said below
- counts: int32 [16], P('slab'), may hold values from 384 to 512, as said below
- gamma: float32 [16], P('head'), may hold values from 0.05 to 1
Outputs:
- query_grads: bfloat16 [8192, 1024], P('slab', 'head')
- key_value_grads: bfloat16 [8192, 4096], P('slab', 'head')
- position_grads: float32 [3, 8192], P(None, 'slab')
Inputs may be any that keep to these rules, and one draw needn't show every extreme that they name: `positions`: row 0 is x within the atom's own slab, from 0 to 1; rows 1 and 2 are y and z, from 0 to 4. `counts`: real atoms fill the first rows of their slab; some slab holds exactly 512 real atoms in every draw.
All inputs are finite; a program needn't handle non-finite values.
Results may differ from a plain program's by a relative error of at most 0.01.
Values may be sent and summed in bfloat16 or wider, within the bound.
A program may use at most 256 MiB of HBM per device.

v0:
```python
import jax
import jax.numpy as jnp
from jax import lax
from jax.sharding import PartitionSpec as P

HEAD_DIM = 64
VEC = 32


score_scale = 0.125
radius_factor = 0.25
envelope_rate = 0.5
negative_fill = -1e30


def passed_along(block, axis, distance):
    devices = range(lax.axis_size(axis))
    route = [((i - distance) % len(devices), i) for i in devices]
    return lax.ppermute(block, axis, route)


def cross_dot(first_op, second_op):
    return lax.dot_general(
        first_op, second_op, (((1,), (1,)), ((), ())), preferred_element_type=jnp.float32
    )


def back_dot(first_op, second_op):
    return lax.dot_general(
        first_op, second_op, (((0,), (0,)), ((), ())), preferred_element_type=jnp.float32
    )


def prime_values(key_block, key_coords, offset):
    values = key_block[:, HEAD_DIM:].astype(jnp.float32)
    gate_values = values[:, HEAD_DIM + 3 * VEC :]
    frames = (key_coords[0] + offset, key_coords[1], key_coords[2])
    pieces = [values[:, :HEAD_DIM]]
    for component in range(3):
        column = HEAD_DIM + component * VEC
        pieces.append(values[:, column : column + VEC] + frames[component][:, None] * gate_values)
    pieces.append(gate_values)
    return jnp.concatenate(pieces, axis=1).astype(jnp.bfloat16)


def prime_grads(cotangent_rows, coords):
    values = cotangent_rows.astype(jnp.float32)
    gate_tail = jnp.zeros((values.shape[0], VEC), jnp.float32)
    for component in range(3):
        column = HEAD_DIM + component * VEC
        gate_tail = gate_tail - coords[component][:, None] * values[:, column : column + VEC]
    joined = jnp.concatenate([values, gate_tail], axis=1) * coords[3][:, None]
    return joined.astype(jnp.bfloat16)


def geometry(query_coords, key_coords, offset):
    shift_x = (key_coords[0] + offset)[None, :] - query_coords[0][:, None]
    shift_y = key_coords[1][None, :] - query_coords[1][:, None]
    shift_z = key_coords[2][None, :] - query_coords[2][:, None]
    distance = shift_x * shift_x + shift_y * shift_y + shift_z * shift_z
    inside = 1.0 - distance * radius_factor
    pair_mask = (inside > 0.0) & (key_coords[3][None, :] > 0.5)
    return (distance, inside, pair_mask)


def pair_scores(query_rows, key_rows, head_gamma, distance):
    return cross_dot(query_rows, key_rows) * score_scale - head_gamma * distance


def head_terms(query_rows, query_coords, cotangent, blocks, head_gamma):
    row_count = query_rows.shape[0]
    row_max = jnp.full((row_count,), negative_fill, jnp.float32)
    for offset, key_rows, primed, key_coords in blocks:
        distance, inside, pair_mask = geometry(query_coords, key_coords, offset)
        scores = pair_scores(query_rows, key_rows, head_gamma, distance)
        row_max = jnp.maximum(row_max, jnp.max(jnp.where(pair_mask, scores, negative_fill), axis=1))
    totals = 1.0 - query_coords[3]
    weighted = jnp.zeros((row_count,), jnp.float32)
    for offset, key_rows, primed, key_coords in blocks:
        distance, inside, pair_mask = geometry(query_coords, key_coords, offset)
        scores = pair_scores(query_rows, key_rows, head_gamma, distance)
        exponent = jnp.where(pair_mask, jnp.exp(scores - row_max[:, None]), 0.0)
        weight = inside * inside * exponent
        totals = totals + jnp.sum(weight, axis=1)
        weighted = weighted + jnp.sum(weight * cross_dot(cotangent, primed), axis=1)
    deltas = weighted / totals
    recip = 1.0 / totals
    query_grad = jnp.zeros((row_count, HEAD_DIM), jnp.float32)
    query_pos = jnp.zeros((3, row_count), jnp.float32)
    gate_sum = jnp.zeros((row_count, VEC), jnp.float32)
    block_terms = []
    gate_start = HEAD_DIM + 3 * VEC
    for offset, key_rows, primed, key_coords in blocks:
        distance, inside, pair_mask = geometry(query_coords, key_coords, offset)
        scores = pair_scores(query_rows, key_rows, head_gamma, distance)
        exponent = jnp.where(pair_mask, jnp.exp(scores - row_max[:, None]), 0.0)
        weight = inside * inside * exponent
        spread = cross_dot(cotangent, primed) - deltas[:, None]
        attend = weight * recip[:, None]
        dscore = attend * spread
        pulling = -head_gamma * dscore - envelope_rate * inside * exponent * recip[:, None] * spread
        dscore_b = dscore.astype(jnp.bfloat16)
        attend_b = attend.astype(jnp.bfloat16)
        query_grad = query_grad + jnp.dot(dscore_b, key_rows, preferred_element_type=jnp.float32)
        key_grad = back_dot(dscore_b, query_rows) * score_scale
        primed_grad = back_dot(attend_b, cotangent)
        gate_values = primed[:, gate_start:]
        gate_sum = gate_sum + jnp.dot(attend_b, gate_values, preferred_element_type=jnp.float32)
        frames = jnp.stack([key_coords[0] + offset, key_coords[1], key_coords[2]])
        row_pull = jnp.sum(pulling, axis=1)
        col_pull = jnp.sum(pulling, axis=0)
        query_side = jnp.einsum("ij,cj->ci", pulling, frames, precision=lax.Precision.HIGHEST)
        key_side = jnp.einsum(
            "ij,ci->cj", pulling, query_coords[:3], precision=lax.Precision.HIGHEST
        )
        query_pos = query_pos - 2.0 * (query_side - query_coords[:3] * row_pull[None, :])
        gate_float = gate_values.astype(jnp.float32)
        value_pos = []
        gate_grad = primed_grad[:, gate_start:]
        for component in range(3):
            column = HEAD_DIM + component * VEC
            piece = primed_grad[:, column : column + VEC]
            value_pos.append(jnp.sum(gate_float * piece, axis=1))
            gate_grad = gate_grad + frames[component][:, None] * piece
        key_pos = 2.0 * (frames * col_pull[None, :] - key_side) + jnp.stack(value_pos)
        view_term = jnp.concatenate([key_grad, primed_grad[:, :gate_start], gate_grad], axis=1)
        block_terms.append((view_term, key_pos))
    cot_float = cotangent.astype(jnp.float32)
    extra = []
    for component in range(3):
        column = HEAD_DIM + component * VEC
        extra.append(jnp.sum(cot_float[:, column : column + VEC] * gate_sum, axis=1))
    query_pos = query_pos - jnp.stack(extra)
    return (query_grad * score_scale, query_pos, block_terms, (row_max, deltas, totals))


def per_device(queries, key_values, out_grads, positions, counts, gamma):
    row_count = queries.shape[0]
    head_count = gamma.shape[0]
    block_width = 2 * HEAD_DIM + 4 * VEC
    cot_width = HEAD_DIM + 3 * VEC
    validity = (jnp.arange(row_count, dtype=jnp.int32) < counts[0]).astype(jnp.float32)
    own_coords = jnp.concatenate([positions, validity[None, :]], axis=0)
    fetched = {0: (key_values, own_coords)}
    for shift_by in (1, -1, 2, -2):
        moved_block = passed_along(key_values, "slab", shift_by)
        placed = passed_along(own_coords, "slab", shift_by)
        fetched[-shift_by] = (moved_block, placed)
    offsets = (-2, -1, 0, 1, 2)
    query_parts = []
    cot_parts = []
    stat_parts = []
    view_parts = {offset: [] for offset in offsets}
    key_pos_sum = {offset: jnp.zeros((3, row_count), jnp.float32) for offset in offsets}
    query_pos_sum = jnp.zeros((3, row_count), jnp.float32)
    for head_index in range(head_count):
        query_rows = queries[:, head_index * HEAD_DIM : (head_index + 1) * HEAD_DIM]
        cotangent = prime_grads(
            out_grads[:, head_index * cot_width : (head_index + 1) * cot_width], own_coords
        )
        blocks = []
        for offset in offsets:
            key_block = fetched[offset][0][
                :, head_index * block_width : (head_index + 1) * block_width
            ]
            key_coords = fetched[offset][1]
            blocks.append(
                (
                    offset,
                    key_block[:, :HEAD_DIM],
                    prime_values(key_block, key_coords, offset),
                    key_coords,
                )
            )
        query_grad, query_pos, block_terms, row_stats = head_terms(
            query_rows, own_coords, cotangent, blocks, gamma[head_index]
        )
        query_parts.append(query_grad.astype(jnp.bfloat16))
        cot_parts.append(cotangent)
        stat_parts.extend(row_stats)
        query_pos_sum = query_pos_sum + query_pos
        for offset, (view_term, key_pos) in zip(offsets, block_terms):
            view_parts[offset].append(view_term)
            key_pos_sum[offset] = key_pos_sum[offset] + key_pos
    view_terms = {offset: jnp.concatenate(view_parts[offset], axis=1) for offset in offsets}
    collected = view_terms[0]
    pos_total = query_pos_sum + key_pos_sum[0]
    for direction in (1, -1):
        moving = (view_terms[2 * direction], key_pos_sum[2 * direction])
        for hop_count in (1, 2):
            moving = passed_along((moving[0], moving[1]), "slab", direction)
            if hop_count == 1:
                moving = (moving[0] + view_terms[direction], moving[1] + key_pos_sum[direction])
        collected = collected + moving[0]
        pos_total = pos_total + moving[1]
    position_grads = lax.psum(pos_total, "head")
    query_grads = jnp.concatenate(query_parts, axis=1)
    return (query_grads, collected.astype(jnp.bfloat16), position_grads)


def solution(mesh):
    in_specs = (
        P("slab", "head"),
        P("slab", "head"),
        P("slab", "head"),
        P(None, "slab"),
        P("slab"),
        P("head"),
    )
    out_specs = (P("slab", "head"), P("slab", "head"), P(None, "slab"))
    return jax.shard_map(
        per_device, mesh=mesh, in_specs=in_specs, out_specs=out_specs, check_vma=False
    )
```

profile of v0, /device:TPU:30, one launch (start us, length us, event | category | flops | bytes accessed | tf_op | source)
XLA Modules:
  0.0 1028.0 jit_solution(973763422364379075)
XLA Ops:
  3.8 4.2 collective-permute-start
  8.0 3.9 copy.9
  77.8 3.9 fusion.1152
  168.9 73.0 %collective-permute-done.3 = bf16[512,2048]{0,1:T(8,128)(2,1)S(1)} collective-permute-done((bf16[512,2048]{0,1:T(8,128)(2,1)S(1)}, bf16[512,2048]{0,1:T(8,128)(2,1)S(1)}, u32[]{:S(2)}, u32[]{:S(2)}) %collective-permute-start.3) | collective-permute-done | bytes 2097184 | tf_op jit(solution)/shard_map/ppermute | solution.py:19
  261.3 4.6 select_reduce_fusion.4
  266.0 4.1 multiply_reduce_fusion.2
  290.7 4.3 multiply_reduce_fusion
  303.4 3.8 multiply_reduce_fusion.3
  321.6 4.2 multiply_reduce_fusion.4
  329.8 3.8 multiply_reduce_fusion.9
  333.6 3.8 multiply_reduce_fusion.8
  337.4 4.0 multiply_reduce_fusion.6
  341.5 4.9 multiply_reduce_fusion.7
  378.4 4.8 fusion.1115
  403.6 4.7 fusion.1114
  442.9 4.3 multiply_reduce_fusion.12
  447.3 4.6 multiply_reduce_fusion.10
  452.0 4.0 multiply_reduce_fusion.14
  455.9 3.8 multiply_reduce_fusion.13
  459.7 4.0 multiply_reduce_fusion.11
  501.4 4.5 fusion.1117
  526.1 4.9 fusion.1116
  557.2 5.0 fusion.1121
  575.5 5.2 fusion.1120
  626.8 4.8 fusion.1119
  649.9 5.4 fusion.1118
  909.9 5.2 add.2623
  916.4 5.2 add.2573
  944.7 4.5 collective-permute-start.13
  952.4 61.6 %collective-permute-done.13 = f32[3,512]{1,0:T(4,128)S(1)} collective-permute-done((f32[3,512]{1,0:T(4,128)S(1)}, f32[3,512]{1,0:T(4,128)S(1)}, u32[]{:S(2)}, u32[]{:S(2)}) %collective-permute-start.13) | collective-permute-done | bytes 6176 | tf_op jit(solution)/shard_map/ppermute | solution.py:19
  1014.0 5.6 psum.7
  1019.6 5.9 add_convert_fusion
  (1630 shorter events, 744.5 us)
Async XLA Ops:
  2.8 144.1 %collective-permute-start.6 = (f32[4,512]{1,0:T(4,128)}, f32[4,512]{1,0:T(4,128)}, u32[]{:S(2)}, u32[]{:S(2)}) collective-permute-start(f32[4,512]{1,0:T(4,128)} %pad_maximum_fusion), channel_id=1, source_target_pairs={{4,0},{6,2},{8,4},{10,6},{12,8},{14,10},{16,12},{18,14},{20,16},{2... | collective-permute-start | bytes 24584 | tf_op jit(solution)/shard_map/ppermute | solution.py:19
  3.3 146.3 %collective-permute-start.4 = (f32[4,512]{1,0:T(4,128)}, f32[4,512]{1,0:T(4,128)}, u32[]{:S(2)}, u32[]{:S(2)}) collective-permute-start(f32[4,512]{1,0:T(4,128)} %pad_maximum_fusion), channel_id=1, source_target_pairs={{2,0},{4,2},{6,4},{8,6},{10,8},{12,10},{14,12},{16,14},{18,16},{20... | collective-permute-start | bytes 24584 | tf_op jit(solution)/shard_map/ppermute | solution.py:19
  3.8 148.3 %collective-permute-start.2 = (f32[4,512]{1,0:T(4,128)}, f32[4,512]{1,0:T(4,128)}, u32[]{:S(2)}, u32[]{:S(2)}) collective-permute-start(f32[4,512]{1,0:T(4,128)} %pad_maximum_fusion), channel_id=1, source_target_pairs={{30,0},{0,2},{2,4},{4,6},{6,8},{8,10},{10,12},{12,14},{14,16},{16,... | collective-permute-start | bytes 24584 | tf_op jit(solution)/shard_map/ppermute | solution.py:19
  3.8 149.8 %collective-permute-start = (f32[4,512]{1,0:T(4,128)}, f32[4,512]{1,0:T(4,128)}, u32[]{:S(2)}, u32[]{:S(2)}) collective-permute-start(f32[4,512]{1,0:T(4,128)} %pad_maximum_fusion), channel_id=1, source_target_pairs={{28,0},{30,2},{0,4},{2,6},{4,8},{6,10},{8,12},{10,14},{12,16},{14,... | collective-permute-start | bytes 24584 | tf_op jit(solution)/shard_map/ppermute | solution.py:19
  11.9 151.2 %collective-permute-start.1 = (bf16[512,2048]{0,1:T(8,128)(2,1)}, bf16[512,2048]{0,1:T(8,128)(2,1)}, u32[]{:S(2)}, u32[]{:S(2)}) collective-permute-start(bf16[512,2048]{0,1:T(8,128)(2,1)} %copy.9), channel_id=1, source_target_pairs={{28,0},{30,2},{0,4},{2,6},{4,8},{6,10},{8,12},{10,14},{12,16},{14,... | collective-permute-start | bytes 6291464 | tf_op jit(solution)/shard_map/ppermute | solution.py:19
  146.9 102.9 %collective-permute-start.7 = (bf16[512,2048]{0,1:T(8,128)(2,1)S(1)}, bf16[512,2048]{0,1:T(8,128)(2,1)S(1)}, u32[]{:S(2)}, u32[]{:S(2)}) collective-permute-start(bf16[512,2048]{0,1:T(8,128)(2,1)S(1)} %copy-done.6), channel_id=1, source_target_pairs={{4,0},{6,2},{8,4},{10,6},{12,8},{14,10},{16,12},{18,14},{20,16},{2... | collective-permute-start | bytes 6291464 | tf_op jit(solution)/shard_map/ppermute | solution.py:19
  149.5 96.1 %collective-permute-start.5 = (bf16[512,2048]{0,1:T(8,128)(2,1)S(1)}, bf16[512,2048]{0,1:T(8,128)(2,1)S(1)}, u32[]{:S(2)}, u32[]{:S(2)}) collective-permute-start(bf16[512,2048]{0,1:T(8,128)(2,1)S(1)} %copy-done.6), channel_id=1, source_target_pairs={{2,0},{4,2},{6,4},{8,6},{10,8},{12,10},{14,12},{16,14},{18,16},{20... | collective-permute-start | bytes 6291464 | tf_op jit(solution)/shard_map/ppermute | solution.py:19
  152.1 89.8 %collective-permute-start.3 = (bf16[512,2048]{0,1:T(8,128)(2,1)S(1)}, bf16[512,2048]{0,1:T(8,128)(2,1)S(1)}, u32[]{:S(2)}, u32[]{:S(2)}) collective-permute-start(bf16[512,2048]{0,1:T(8,128)(2,1)S(1)} %copy-done.6), channel_id=1, source_target_pairs={{30,0},{0,2},{2,4},{4,6},{6,8},{8,10},{10,12},{12,14},{14,16},{16,... | collective-permute-start | bytes 6291464 | tf_op jit(solution)/shard_map/ppermute | solution.py:19
  258.6 303.8 %copy-start.46 = (f32[512,512]{0,1:T(8,128)}, f32[512,512]{0,1:T(8,128)S(1)}, u32[]{:S(2)}) copy-start(f32[512,512]{0,1:T(8,128)S(1)} %fusion.38) | copy-start | bytes 3145732
  261.2 305.9 %copy-start.50 = (f32[512,512]{0,1:T(8,128)}, f32[512,512]{0,1:T(8,128)S(1)}, u32[]{:S(2)}) copy-start(f32[512,512]{0,1:T(8,128)S(1)} %get-tuple-element.909) | copy-start | bytes 3145732
  265.9 306.2 %copy-start.48 = (f32[512,512]{0,1:T(8,128)}, f32[512,512]{0,1:T(8,128)S(1)}, u32[]{:S(2)}) copy-start(f32[512,512]{0,1:T(8,128)S(1)} %get-tuple-element.908) | copy-start | bytes 3145732
  271.2 362.9 %copy-start.54 = (f32[512,512]{0,1:T(8,128)}, f32[512,512]{0,1:T(8,128)S(1)}, u32[]{:S(2)}) copy-start(f32[512,512]{0,1:T(8,128)S(1)} %fusion.28) | copy-start | bytes 3145732
  272.5 215.9 %copy-start.58 = (f32[512,512]{0,1:T(8,128)}, f32[512,512]{0,1:T(8,128)S(1)}, u32[]{:S(2)}) copy-start(f32[512,512]{0,1:T(8,128)S(1)} %fusion.23) | copy-start | bytes 3145732
  273.7 232.1 %copy-start.73 = (f32[512,512]{0,1:T(8,128)}, f32[512,512]{0,1:T(8,128)S(1)}, u32[]{:S(2)}) copy-start(f32[512,512]{0,1:T(8,128)S(1)} %fusion.18) | copy-start | bytes 3145732
  274.8 256.2 %copy-start.75 = (f32[512,512]{0,1:T(8,128)}, f32[512,512]{0,1:T(8,128)S(1)}, u32[]{:S(2)}) copy-start(f32[512,512]{0,1:T(8,128)S(1)} %fusion.13) | copy-start | bytes 3145732
  277.2 305.3 %copy-start.52 = (f32[512,512]{0,1:T(8,128)}, f32[512,512]{0,1:T(8,128)S(1)}, u32[]{:S(2)}) copy-start(f32[512,512]{0,1:T(8,128)S(1)} %fusion.33) | copy-start | bytes 3145732
  296.1 175.3 %copy-start.63 = (f32[512,512]{0,1:T(8,128)}, f32[512,512]{0,1:T(8,128)S(1)}, u32[]{:S(2)}) copy-start(f32[512,512]{0,1:T(8,128)S(1)} %fusion.26) | copy-start | bytes 3145732
  297.4 186.2 %copy-start.69 = (f32[512,512]{0,1:T(8,128)}, f32[512,512]{0,1:T(8,128)S(1)}, u32[]{:S(2)}) copy-start(f32[512,512]{0,1:T(8,128)S(1)} %fusion.21) | copy-start | bytes 3145732
  302.1 285.3 %copy-start.56 = (f32[512,512]{0,1:T(8,128)}, f32[512,512]{0,1:T(8,128)S(1)}, u32[]{:S(2)}) copy-start(f32[512,512]{0,1:T(8,128)S(1)} %fusion.31) | copy-start | bytes 3145732
  311.3 179.9 %copy-start.71 = (f32[512,512]{0,1:T(8,128)}, f32[512,512]{0,1:T(8,128)S(1)}, u32[]{:S(2)}) copy-start(f32[512,512]{0,1:T(8,128)S(1)} %fusion.20) | copy-start | bytes 3145732
  341.5 200.0 %copy-start.308 = (f32[512]{0:T(512)}, f32[512]{0:T(512)S(1)}, u32[]{:S(2)}) copy-start(f32[512]{0:T(512)S(1)} %maximum_maximum_fusion.5) | copy-start | bytes 6148
  383.2 215.6 %copy-start.21 = (bf16[512,512]{0,1:T(8,128)(2,1)}, bf16[512,512]{0,1:T(8,128)(2,1)S(1)}, u32[]{:S(2)}) copy-start(bf16[512,512]{0,1:T(8,128)(2,1)S(1)} %get-tuple-element.748) | copy-start | bytes 1572868
  494.2 197.5 %copy-start.292 = (f32[512]{0:T(512)}, f32[512]{0:T(512)S(1)}, u32[]{:S(2)}) copy-start(f32[512]{0:T(512)S(1)} %get-tuple-element.931) | copy-start | bytes 6148
  494.2 200.9 %copy-start.294 = (f32[512]{0:T(512)}, f32[512]{0:T(512)S(1)}, u32[]{:S(2)}) copy-start(f32[512]{0:T(512)S(1)} %get-tuple-element.466) | copy-start | bytes 6148
  769.7 173.9 %collective-permute-start.12 = (f32[3,512]{1,0:T(4,128)}, f32[3,512]{1,0:T(4,128)}, u32[]{:S(2)}, u32[]{:S(2)}) collective-permute-start(f32[3,512]{1,0:T(4,128)} %fusion.879), channel_id=1, source_target_pairs={{30,0},{0,2},{2,4},{4,6},{6,8},{8,10},{10,12},{12,14},{14,16},{16,... | collective-permute-start | bytes 18440 | tf_op jit(solution)/shard_map/ppermute | solution.py:19
  806.6 142.6 %collective-permute-start.14 = (f32[3,512]{1,0:T(4,128)}, f32[3,512]{1,0:T(4,128)}, u32[]{:S(2)}, u32[]{:S(2)}) collective-permute-start(f32[3,512]{1,0:T(4,128)} %fusion.894), channel_id=1, source_target_pairs={{2,0},{4,2},{6,4},{8,6},{10,8},{12,10},{14,12},{16,14},{18,16},{20... | collective-permute-start | bytes 18440 | tf_op jit(solution)/shard_map/ppermute | solution.py:19
  808.3 101.6 %collective-permute-start.10 = (f32[512,2048]{0,1:T(8,128)}, f32[512,2048]{0,1:T(8,128)}, u32[]{:S(2)}, u32[]{:S(2)}) collective-permute-start(f32[512,2048]{0,1:T(8,128)} %get-tuple-element.692), channel_id=1, source_target_pairs={{2,0},{4,2},{6,4},{8,6},{10,8},{12,10},{14,12},{16,14},{18,16},{20... | collective-permute-start | bytes 12582920 | tf_op jit(solution)/shard_map/ppermute | solution.py:19
  808.4 108.0 %collective-permute-start.8 = (f32[512,2048]{0,1:T(8,128)}, f32[512,2048]{0,1:T(8,128)}, u32[]{:S(2)}, u32[]{:S(2)}) collective-permute-start(f32[512,2048]{0,1:T(8,128)} %get-tuple-element.668), channel_id=1, source_target_pairs={{30,0},{0,2},{2,4},{4,6},{6,8},{8,10},{10,12},{12,14},{14,16},{16,... | collective-permute-start | bytes 12582920 | tf_op jit(solution)/shard_map/ppermute | solution.py:19
  915.1 104.5 %collective-permute-start.11 = (f32[512,2048]{0,1:T(8,128)}, f32[512,2048]{0,1:T(8,128)}, u32[]{:S(2)}, u32[]{:S(2)}) collective-permute-start(f32[512,2048]{0,1:T(8,128)} %add.2623), channel_id=1, source_target_pairs={{2,0},{4,2},{6,4},{8,6},{10,8},{12,10},{14,12},{16,14},{18,16},{20... | collective-permute-start | bytes 12582920 | tf_op jit(solution)/shard_map/ppermute | solution.py:19
  921.6 98.0 %collective-permute-start.9 = (f32[512,2048]{0,1:T(8,128)}, f32[512,2048]{0,1:T(8,128)}, u32[]{:S(2)}, u32[]{:S(2)}) collective-permute-start(f32[512,2048]{0,1:T(8,128)} %add.2573), channel_id=1, source_target_pairs={{30,0},{0,2},{2,4},{4,6},{6,8},{8,10},{10,12},{12,14},{14,16},{16,... | collective-permute-start | bytes 12582920 | tf_op jit(solution)/shard_map/ppermute | solution.py:19
  944.7 69.2 %collective-permute-start.13 = (f32[3,512]{1,0:T(4,128)S(1)}, f32[3,512]{1,0:T(4,128)S(1)}, u32[]{:S(2)}, u32[]{:S(2)}) collective-permute-start(f32[3,512]{1,0:T(4,128)S(1)} %fusion.887), channel_id=1, source_target_pairs={{30,0},{0,2},{2,4},{4,6},{6,8},{8,10},{10,12},{12,14},{14,16},{16,... | collective-permute-start | bytes 18440 | tf_op jit(solution)/shard_map/ppermute | solution.py:19
  950.2 63.7 %collective-permute-start.15 = (f32[3,512]{1,0:T(4,128)S(1)}, f32[3,512]{1,0:T(4,128)S(1)}, u32[]{:S(2)}, u32[]{:S(2)}) collective-permute-start(f32[3,512]{1,0:T(4,128)S(1)} %fusion.902), channel_id=1, source_target_pairs={{2,0},{4,2},{6,4},{8,6},{10,8},{12,10},{14,12},{16,14},{18,16},{20... | collective-permute-start | bytes 18440 | tf_op jit(solution)/shard_map/ppermute | solution.py:19
  (490 other events, 5597.8 us)
where the time goes:
time: 1050 us; the launch traced here: 1030 us
  matrix products  484 us (46%)
  other arithmetic  220 us (21%)
  local copies, waits for them, and re-layouts  152 us (14%)
  waiting for transfers between devices  135 us (13%)
  starting transfers between devices  18.7 us (2%)
  between operations  13.1 us (1%)
    dot_general x80, matrix products, cross_dot(): lax.dot_general(first_op, second_op, (((1,), (1,)), ((), ())), preferred_...  148 us
    ppermute x16, waiting for transfers between devices, passed_along(): return lax.ppermute(block, axis, route)  135 us
    dot_general x80, matrix products, back_dot(): lax.dot_general(first_op, second_op, (((0,), (0,)), ((), ())), preferred_...  131 us
    dot_general x40, matrix products, head_terms(): jnp.dot(attend_b, gate_values, preferred_element_type=jnp.float32)  74.3 us
    reduce_sum x16, other arithmetic, head_terms(): col_pull = jnp.sum(pulling, axis=0)  62.4 us
    dot_general x40, matrix products, head_terms(): jnp.einsum('ij,ci->cj', pulling, query_coords[:3], precision=lax.Precisio...  61.6 us
    unnamed x1067, local copies, waits for them, and re-layouts  55 us
    reduce_sum x40, other arithmetic, head_terms(): value_pos.append(jnp.sum(gate_float * piece, axis=1))  52.5 us
  transfers between devices with their start and end apart: 16, of which 2 were waited for; matrix products, arithmetic and copies ran while one was open for 32% of the time, Pallas kernels for 0%

commit v1 on v0

v1 whole, which is shorter than its diff:
```python
import functools

import jax
import jax.numpy as jnp
from jax import lax
from jax.experimental import pallas as pl
from jax.experimental.pallas import tpu as pltpu
from jax.sharding import PartitionSpec as P

HEAD_DIM = 64
VEC = 32
WIDTH = 2 * HEAD_DIM + 4 * VEC
COT = HEAD_DIM + 3 * VEC
OFFSETS = (-2, -1, 0, 1, 2)
FAR = 1e6
FLOOR = -1e4
CHUNK = 256
GROUPS = 2


def passed_along(block, axis, distance):
    count = lax.axis_size(axis)
    route = [((i - distance) % count, i) for i in range(count)]
    return lax.ppermute(block, axis, route)


def dot_nt(a, b):
    return lax.dot_general(a, b, (((1,), (1,)), ((), ())), preferred_element_type=jnp.float32)


def dot_tn(a, b):
    return lax.dot_general(a, b, (((0,), (0,)), ((), ())), preferred_element_type=jnp.float32)


def dot_nn(a, b):
    return jnp.dot(a, b, preferred_element_type=jnp.float32)


def spread_groups(x):
    x = x + pltpu.roll(x, 2 * VEC, 1)
    return x + pltpu.roll(x, VEC, 1)


def folded(x):
    return jnp.sum(x.reshape(x.shape[0] // 8, 8, x.shape[1]), axis=0)


def kernel(gamma_ref, q_ref, c_ref, ct_ref, qc_ref, kc_ref, *rest):
    views = len(OFFSETS)
    kv_refs = rest[:views]
    t_refs = rest[views : 2 * views]
    dq_ref, kp_ref, qp_ref = rest[2 * views : 2 * views + 3]
    dist, pair, dpair, pull, gates, frames, vpos, qpos = rest[2 * views + 3 :]
    rows = q_ref.shape[1]
    chunks = rows // CHUNK
    step = pl.program_id(0)
    head_gamma = gamma_ref[step]
    lane = lax.broadcasted_iota(jnp.int32, (CHUNK, 4 * VEC), 1)
    last_group = lane >= 3 * VEC

    @pl.when(step == 0)
    def _():
        vpos[...] = jnp.zeros_like(vpos)
        qpos[...] = jnp.zeros_like(qpos)

        @pl.loop(0, views * chunks)
        def _(k):
            at = pl.ds(pl.multiple_of(k * CHUNK, CHUNK), CHUNK)
            kc = kc_ref[at, :]
            total = None
            for c in range(3):
                shift = kc[:, c : c + 1] - qc_ref[c : c + 1, :]
                total = shift * shift if total is None else total + shift * shift
            counted = (1.0 - total * 0.25 > 0.0) & (kc[:, 3:4] > 0.5)
            dist[at, :] = jnp.where(counted, total, FAR)
            pull[at, :] = jnp.zeros((CHUNK, rows), jnp.float32)
            frames[at, :] = jnp.where(
                lane < VEC,
                kc[:, 0:1],
                jnp.where(lane < 2 * VEC, kc[:, 1:2], jnp.where(last_group, 0.0, kc[:, 2:3])),
            )

    q = q_ref[0]
    cot = c_ref[0]
    peak = jnp.full((8, rows), FLOOR, jnp.float32)
    for v in range(views):

        def scored(k, peak, v=v):
            off = pl.multiple_of(k * CHUNK, CHUNK)
            at = pl.ds(v * rows + off, CHUNK)
            s = dot_nt(kv_refs[v][pl.ds(off, CHUNK), : 2 * HEAD_DIM], q[:, : 2 * HEAD_DIM])
            s = s - head_gamma * dist[at, :]
            pair[at, :] = s
            return jnp.maximum(peak, jnp.max(s.reshape(CHUNK // 8, 8, rows), axis=0))

        peak = lax.fori_loop(0, chunks, scored, peak, unroll=True)
    peak = jnp.max(peak, axis=0, keepdims=True)

    totals = jnp.zeros((8, rows), jnp.float32)
    weighted = jnp.zeros((8, rows), jnp.float32)
    for v in range(views):

        def summed(k, carry, v=v):
            totals, weighted = carry
            off = pl.multiple_of(k * CHUNK, CHUNK)
            at = pl.ds(v * rows + off, CHUNK)
            kv = kv_refs[v][pl.ds(off, CHUNK), :]
            high = kv[:, 2 * HEAD_DIM :].astype(jnp.float32)
            gate = spread_groups(jnp.where(last_group, high, 0.0))
            gates[at, :] = gate
            primed = (high + frames[at, :] * gate).astype(jnp.bfloat16)
            dp = dot_nt(kv[:, : 2 * HEAD_DIM], cot[:, : 2 * HEAD_DIM]) + dot_nt(
                primed, cot[:, 2 * HEAD_DIM :]
            )
            inside = 1.0 - 0.25 * dist[at, :]
            part = inside * jnp.exp(pair[at, :] - peak)
            pair[at, :] = part
            dpair[at, :] = dp
            weight = inside * part
            return totals + folded(weight), weighted + folded(weight * dp)

        totals, weighted = lax.fori_loop(0, chunks, summed, (totals, weighted), unroll=True)
    total = jnp.sum(totals, axis=0, keepdims=True) + (1.0 - qc_ref[3:4, :])
    recip = 1.0 / total
    delta = jnp.sum(weighted, axis=0, keepdims=True) / total

    dq = jnp.zeros((2 * HEAD_DIM, rows), jnp.float32)
    gsum = jnp.zeros((4 * VEC, rows), jnp.float32)
    for v in range(views):

        def graded(k, carry, v=v):
            dq, gsum = carry
            off = pl.multiple_of(k * CHUNK, CHUNK)
            at = pl.ds(v * rows + off, CHUNK)
            here = pl.ds(off, CHUNK)
            inside = 1.0 - 0.25 * dist[at, :]
            unit = pair[at, :] * recip
            moved = unit * (dpair[at, :] - delta)
            dscore = inside * moved
            pull[at, :] += head_gamma * dscore + 0.5 * moved
            dscore_b = dscore.astype(jnp.bfloat16)
            attend_b = (inside * unit).astype(jnp.bfloat16)
            term = dot_nn(dscore_b, q) + dot_nn(attend_b, cot)
            kv = kv_refs[v][here, :]
            dq = dq + dot_tn(kv[:, : 2 * HEAD_DIM], dscore_b)
            gsum = gsum + dot_tn(kv[:, 2 * HEAD_DIM :], attend_b)
            high = term[:, 2 * HEAD_DIM :]
            vpos[at, :] += gates[at, :] * high
            extra = spread_groups(frames[at, :] * high)
            high = high + jnp.where(last_group, extra, 0.0)
            t_refs[v][here, : 2 * HEAD_DIM] = term[:, : 2 * HEAD_DIM].astype(t_refs[v].dtype)
            t_refs[v][here, 2 * HEAD_DIM :] = high.astype(t_refs[v].dtype)
            return dq, gsum

        dq, gsum = lax.fori_loop(0, chunks, graded, (dq, gsum), unroll=True)
    dq_ref[...] = (dq[:HEAD_DIM, :] * 0.125).astype(dq_ref.dtype)
    gsum = gsum[3 * VEC :, :]
    for c in range(3):
        part = ct_ref[0, c * VEC : (c + 1) * VEC, :].astype(jnp.float32) * gsum
        qpos[c : c + 1, :] -= jnp.sum(part, axis=0, keepdims=True)

    @pl.when(step == pl.num_programs(0) - 1)
    def _():
        def placed(k, sums):
            at = pl.ds(pl.multiple_of(k * CHUNK, CHUNK), CHUNK)
            kc = kc_ref[at, :]
            force = -2.0 * pull[at, :]
            vp = vpos[at, :]
            out = []
            cols = []
            for c in range(3):
                moment = force * (kc[:, c : c + 1] - qc_ref[c : c + 1, :])
                out.append(sums[c] - folded(moment))
                mine = (lane >= c * VEC) & (lane < (c + 1) * VEC)
                col = jnp.sum(moment, axis=1, keepdims=True)
                cols.append(col + jnp.sum(jnp.where(mine, vp, 0.0), axis=1, keepdims=True))
            kp_ref[at, :] = jnp.concatenate(cols + [jnp.zeros_like(cols[0])], axis=1)
            return tuple(out)

        zero = jnp.zeros((8, rows), jnp.float32)
        sums = lax.fori_loop(0, views * chunks, placed, (zero, zero, zero))
        qp_ref[...] = qpos[...]
        for c in range(3):
            qp_ref[c : c + 1, :] += jnp.sum(sums[c], axis=0, keepdims=True)


def head_group(gamma, q, cot, cot_t, query_coords, key_coords, blocks):
    heads, rows, _ = q.shape
    views = len(OFFSETS)
    keys = views * rows
    f32 = jnp.float32
    per_head = lambda h: (h, 0, 0)
    whole = lambda h: (0, 0)
    column = lambda h: (0, h)
    return pl.pallas_call(
        kernel,
        grid=(heads,),
        in_specs=[
            pl.BlockSpec(memory_space=pltpu.SMEM),
            pl.BlockSpec((1, rows, WIDTH), per_head),
            pl.BlockSpec((1, rows, WIDTH), per_head),
            pl.BlockSpec((1, 3 * VEC, rows), per_head),
            pl.BlockSpec(query_coords.shape, whole),
            pl.BlockSpec(key_coords.shape, whole),
        ]
        + [pl.BlockSpec((rows, WIDTH), column)] * views,
        out_specs=[pl.BlockSpec((rows, WIDTH), column)] * views
        + [
            pl.BlockSpec((HEAD_DIM, rows), lambda h: (h, 0)),
            pl.BlockSpec((keys, 4), whole),
            pl.BlockSpec((8, rows), whole),
        ],
        out_shape=[jax.ShapeDtypeStruct((rows, heads * WIDTH), jnp.bfloat16)] * views
        + [
            jax.ShapeDtypeStruct((heads * HEAD_DIM, rows), jnp.bfloat16),
            jax.ShapeDtypeStruct((keys, 4), f32),
            jax.ShapeDtypeStruct((8, rows), f32),
        ],
        scratch_shapes=[
            pltpu.VMEM((keys, rows), f32),
            pltpu.VMEM((keys, rows), f32),
            pltpu.VMEM((keys, rows), f32),
            pltpu.VMEM((keys, rows), f32),
            pltpu.VMEM((keys, 4 * VEC), f32),
            pltpu.VMEM((keys, 4 * VEC), f32),
            pltpu.VMEM((keys, 4 * VEC), f32),
            pltpu.VMEM((8, rows), f32),
        ],
        compiler_params=pltpu.CompilerParams(
            dimension_semantics=("arbitrary",), vmem_limit_bytes=60 * 2**20
        ),
        cost_estimate=pl.CostEstimate(
            flops=heads * rows * keys * 1500,
            bytes_accessed=heads * keys * WIDTH * 4,
            transcendentals=heads * rows * keys,
        ),
        name="pairs",
    )(gamma, q, cot, cot_t, query_coords, key_coords, *blocks)


def per_device(queries, key_values, out_grads, positions, counts, gamma):
    rows = queries.shape[0]
    heads = gamma.shape[0]
    groups = GROUPS if heads % GROUPS == 0 else 1
    size = heads // groups
    f32 = jnp.float32
    bf16 = jnp.bfloat16
    validity = (jnp.arange(rows, dtype=jnp.int32) < counts[0]).astype(f32)
    coords = jnp.concatenate([positions, validity[None, :]], axis=0)
    coords_at = {0: coords}
    for o in (1, -1, 2, -2):
        coords_at[o] = passed_along(coords, "slab", -o)

    pieces = [key_values[:, g * size * WIDTH : (g + 1) * size * WIDTH] for g in range(groups)]
    fetched = []
    for g in range(groups):
        blocks = {0: pieces[g]}
        for o in (1, -1):
            blocks[o] = passed_along(blocks[0], "slab", -o)
        for o in (1, -1):
            blocks[2 * o] = passed_along(blocks[o], "slab", -o)
        fetched.append(blocks)

    q = queries.reshape(rows, heads, HEAD_DIM).transpose(1, 0, 2) * bf16(0.125)
    q = jnp.pad(q, ((0, 0), (0, 0), (0, WIDTH - HEAD_DIM)))
    do = out_grads.reshape(rows, heads, COT).transpose(1, 0, 2).astype(f32)
    tail = jnp.zeros((heads, rows, VEC), f32)
    for c in range(3):
        at = HEAD_DIM + c * VEC
        tail = tail - coords[c][None, :, None] * do[:, :, at : at + VEC]
    cot = jnp.concatenate([do, tail], axis=2) * validity[None, :, None]
    cot = jnp.pad(cot, ((0, 0), (0, 0), (HEAD_DIM, 0))).astype(bf16)
    cot_t = cot[:, :, 2 * HEAD_DIM : 2 * HEAD_DIM + 3 * VEC].transpose(0, 2, 1)

    query_coords = jnp.pad(coords, ((0, 4), (0, 0)))
    key_coords = jnp.concatenate(
        [coords_at[o] + jnp.array([o, 0, 0, 0], f32)[:, None] for o in OFFSETS], axis=1
    ).T

    dq_parts = []
    kv_parts = []
    key_pos = 0.0
    query_pos = 0.0
    for g in range(groups):
        part = slice(g * size, (g + 1) * size)
        out = head_group(
            gamma[part], q[part], cot[part], cot_t[part], query_coords, key_coords,
            [fetched[g][o] for o in OFFSETS],
        )
        terms = dict(zip(OFFSETS, out[: len(OFFSETS)]))
        dq_parts.append(out[-3])
        key_pos = key_pos + out[-2]
        query_pos = query_pos + out[-1][:3]
        collected = terms[0].astype(f32)
        for o in (1, -1):
            moving = passed_along(terms[2 * o], "slab", o)
            moving = (moving.astype(f32) + terms[o].astype(f32)).astype(bf16)
            collected = collected + passed_along(moving, "slab", o).astype(f32)
        kv_parts.append(collected.astype(bf16))

    key_pos = key_pos.T[:3].reshape(3, len(OFFSETS), rows)
    total = query_pos
    for n, o in enumerate(OFFSETS):
        total = total + (key_pos[:, n] if o == 0 else passed_along(key_pos[:, n], "slab", o))
    position_grads = lax.psum(total, "head")
    query_grads = jnp.concatenate(dq_parts, axis=0).T
    return (query_grads, jnp.concatenate(kv_parts, axis=1), position_grads)


def solution(mesh):
    in_specs = (
        P("slab", "head"),
        P("slab", "head"),
        P("slab", "head"),
        P(None, "slab"),
        P("slab"),
        P("head"),
    )
    out_specs = (P("slab", "head"), P("slab", "head"), P(None, "slab"))
    return jax.shard_map(
        per_device, mesh=mesh, in_specs=in_specs, out_specs=out_specs, check_vma=False
    )
```

time: 1050 us -> 278 us (0.26)
  the two profiles are of different devices: /device:TPU:30 before, /device:TPU:0 now
where the time goes in v1:
time: 278 us
  starting transfers between devices  94.4 us (34%)
  Pallas kernels  92.9 us (33%)
  waiting for transfers between devices  47.8 us (17%)
  local copies, waits for them, and re-layouts  21.3 us (8%)
  other arithmetic  14 us (5%)
  blocking collectives  5.59 us (2%)
    ppermute x24, starting transfers between devices, passed_along(): return lax.ppermute(block, axis, route)  94.4 us
    pallas_call x2, Pallas kernels, head_group(): pl.pallas_call(kernel, grid=(heads,), in_specs=[pl.BlockSpec(memory_space...  92.9 us
    ppermute x24, waiting for transfers between devices, passed_along(): return lax.ppermute(block, axis, route)  47.8 us
    psum x1, blocking collectives, per_device(): position_grads = lax.psum(total, 'head')  5.59 us
  transfers between devices with their start and end apart: 24, of which 8 were waited for; matrix products, arithmetic and copies ran while one was open for 10% of the time, Pallas kernels for 33%

profile of v1, /device:TPU:0, one launch (start us, length us, event | category | flops | bytes accessed | tf_op | source)
XLA Modules:
  0.0 277.7 jit_solution(1043808564097350356)
XLA Ops:
  0.6 3.1 %fusion.7 = (bf16[512,1024]{1,0:T(8,128)(2,1)}, bf16[512,1024]{1,0:T(8,128)(2,1)}) fusion(bf16[512,2048]{1,0:T(8,128)(2,1)} %param.12), kind=kLoop, calls=%fused_computation.35 | loop fusion | bytes 4194304 | tf_op jit(solution)/shard_map/slice | solution.py:254
  4.2 5.0 %collective-permute-start.6 = (bf16[512,1024]{1,0:T(8,128)(2,1)}, bf16[512,1024]{1,0:T(8,128)(2,1)}, u32[]{:S(2)}, u32[]{:S(2)}) collective-permute-start(bf16[512,1024]{1,0:T(8,128)(2,1)} %get-tuple-element.44.rest_2_), channel_id=1, source_target_pairs={{2,0},{4,2},{6,4},{8,6},{10,8},{12,10},{14,12},{16,14},{18,16},{20... | collective-permute-start | bytes 3145736 | tf_op jit(solution)/shard_map/ppermute | solution.py:24
  10.7 1.6 copy.38
  16.8 1.5 copy.37
  18.3 2.1 fusion.9
  20.4 1.8 collective-permute-done.4.rest_1_
  22.2 19.3 %collective-permute-start.5 = (bf16[512,1024]{1,0:T(8,128)(2,1)}, bf16[512,1024]{1,0:T(8,128)(2,1)}, u32[]{:S(2)}, u32[]{:S(2)}) collective-permute-start(bf16[512,1024]{1,0:T(8,128)(2,1)} %collective-permute-done.4.rest_1_), channel_id=1, source_target_pairs={{30,0},{0,2},{2,4},{4,6},{6,8},{8,10},{10,12},{12,14},{14,16},{16,... | collective-permute-start | bytes 3145736 | tf_op jit(solution)/shard_map/ppermute | solution.py:24
  41.5 1.6 pad_slice_fusion.1
  46.3 17.6 %collective-permute-start.1 = (f32[4,512]{1,0:T(4,128)S(1)}, f32[4,512]{1,0:T(4,128)S(1)}, u32[]{:S(2)}, u32[]{:S(2)}) collective-permute-start(f32[4,512]{1,0:T(4,128)S(1)} %pad_maximum_fusion.1), channel_id=1, source_target_pairs={{30,0},{0,2},{2,4},{4,6},{6,8},{8,10},{10,12},{12,14},{14,16},{16,... | collective-permute-start | bytes 24584 | tf_op jit(solution)/shard_map/ppermute | solution.py:24
  64.0 6.5 %collective-permute-done.1 = f32[4,512]{1,0:T(4,128)S(1)} collective-permute-done((f32[4,512]{1,0:T(4,128)S(1)}, f32[4,512]{1,0:T(4,128)S(1)}, u32[]{:S(2)}, u32[]{:S(2)}) %collective-permute-start.1) | collective-permute-done | bytes 8224 | tf_op jit(solution)/shard_map/ppermute | solution.py:24
  70.6 5.4 %collective-permute-done.2 = f32[4,512]{1,0:T(4,128)S(1)} collective-permute-done((f32[4,512]{1,0:T(4,128)S(1)}, f32[4,512]{1,0:T(4,128)S(1)}, u32[]{:S(2)}, u32[]{:S(2)}) %collective-permute-start.2) | collective-permute-done | bytes 8224 | tf_op jit(solution)/shard_map/ppermute | solution.py:24
  76.0 6.1 %collective-permute-start.3 = (f32[4,512]{1,0:T(4,128)S(1)}, f32[4,512]{1,0:T(4,128)S(1)}, u32[]{:S(2)}, u32[]{:S(2)}) collective-permute-start(f32[4,512]{1,0:T(4,128)S(1)} %pad_maximum_fusion.1), channel_id=1, source_target_pairs={{4,0},{6,2},{8,4},{10,6},{12,8},{14,10},{16,12},{18,14},{20,16},{2... | collective-permute-start | bytes 24584 | tf_op jit(solution)/shard_map/ppermute | solution.py:24
  82.1 1.4 collective-permute-start.11
  83.7 1.5 copy.39
  85.2 46.5 %pairs.2 = (bf16[512,1024]{1,0:T(8,128)(2,1)}, bf16[512,1024]{1,0:T(8,128)(2,1)}, bf16[512,1024]{1,0:T(8,128)(2,1)}, bf16[512,1024]{1,0:T(8,128)(2,1)}, bf16[512...) custom-call(f32[4]{0:T(128)} %get-tuple-element.60.gamma_ref, ...), custom_call_target="tpu_custom_call" | custom-call | flops 7864320000 | bytes 10485760 | tf_op jit(solution)/shard_map/pairs/pallas_call | solution.py:195
  131.8 4.7 %collective-permute-start.14 = (bf16[512,1024]{1,0:T(8,128)(2,1)}, bf16[512,1024]{1,0:T(8,128)(2,1)S(1)}, u32[]{:S(2)}, u32[]{:S(2)}) collective-permute-start(bf16[512,1024]{1,0:T(8,128)(2,1)} %get-tuple-element.24), channel_id=1, source_target_pairs={{2,0},{4,2},{6,4},{8,6},{10,8},{12,10},{14,12},{16,14},{18,16},{20... | collective-permute-start | bytes 3145736 | tf_op jit(solution)/shard_map/ppermute | solution.py:24
  137.5 46.5 %pairs.3 = (bf16[512,1024]{1,0:T(8,128)(2,1)}, bf16[512,1024]{1,0:T(8,128)(2,1)}, bf16[512,1024]{1,0:T(8,128)(2,1)}, bf16[512,1024]{1,0:T(8,128)(2,1)}, bf16[512...) custom-call(f32[4]{0:T(128)} %get-tuple-element.61.gamma_ref, ...), custom_call_target="tpu_custom_call" | custom-call | flops 7864320000 | bytes 10485760 | tf_op jit(solution)/shard_map/pairs/pallas_call | solution.py:195
  184.0 4.4 %collective-permute-start.18 = (bf16[512,1024]{1,0:T(8,128)(2,1)}, bf16[512,1024]{1,0:T(8,128)(2,1)S(1)}, u32[]{:S(2)}, u32[]{:S(2)}) collective-permute-start(bf16[512,1024]{1,0:T(8,128)(2,1)} %get-tuple-element.29), channel_id=1, source_target_pairs={{2,0},{4,2},{6,4},{8,6},{10,8},{12,10},{14,12},{16,14},{18,16},{20... | collective-permute-start | bytes 3145736 | tf_op jit(solution)/shard_map/ppermute | solution.py:24
  189.4 1.6 add_convert_fusion.5
  191.6 4.5 %collective-permute-start.15 = (bf16[512,1024]{1,0:T(8,128)(2,1)S(1)}, bf16[512,1024]{1,0:T(8,128)(2,1)}, u32[]{:S(2)}, u32[]{:S(2)}) collective-permute-start(bf16[512,1024]{1,0:T(8,128)(2,1)S(1)} %add_convert_fusion.4), channel_id=1, source_target_pairs={{2,0},{4,2},{6,4},{8,6},{10,8},{12,10},{14,12},{16,14},{18,16},{20... | collective-permute-start | bytes 3145736 | tf_op jit(solution)/shard_map/ppermute | solution.py:24
  196.0 5.2 %collective-permute-done.16 = bf16[512,1024]{1,0:T(8,128)(2,1)S(1)} collective-permute-done((bf16[512,1024]{1,0:T(8,128)(2,1)}, bf16[512,1024]{1,0:T(8,128)(2,1)S(1)}, u32[]{:S(2)}, u32[]{:S(2)}) %collective-permute-start.16) | collective-permute-done | bytes 1048608 | tf_op jit(solution)/shard_map/ppermute | solution.py:24
  201.3 1.4 add_convert_fusion.2
  202.6 14.6 %collective-permute-start.17 = (bf16[512,1024]{1,0:T(8,128)(2,1)}, bf16[512,1024]{1,0:T(8,128)(2,1)}, u32[]{:S(2)}, u32[]{:S(2)}) collective-permute-start(bf16[512,1024]{1,0:T(8,128)(2,1)} %add_convert_fusion.2), channel_id=1, source_target_pairs={{30,0},{0,2},{2,4},{4,6},{6,8},{8,10},{10,12},{12,14},{14,16},{16,... | collective-permute-start | bytes 3145736 | tf_op jit(solution)/shard_map/ppermute | solution.py:24
  217.2 1.4 add_convert_fusion.1
  219.0 15.4 %collective-permute-start.20 = (f32[3,512]{1,0:T(4,128)S(1)}, f32[3,512]{1,0:T(4,128)S(1)}, u32[]{:S(2)}, u32[]{:S(2)}) collective-permute-start(f32[3,512]{1,0:T(4,128)S(1)} %bitcast.43), channel_id=1, source_target_pairs={{4,0},{6,2},{8,4},{10,6},{12,8},{14,10},{16,12},{18,14},{20,16},{2... | collective-permute-start | bytes 18440 | tf_op jit(solution)/shard_map/ppermute | solution.py:24
  234.5 17.8 %collective-permute-done.20 = f32[3,512]{1,0:T(4,128)S(1)} collective-permute-done((f32[3,512]{1,0:T(4,128)S(1)}, f32[3,512]{1,0:T(4,128)S(1)}, u32[]{:S(2)}, u32[]{:S(2)}) %collective-permute-start.20) | collective-permute-done | bytes 6176 | tf_op jit(solution)/shard_map/ppermute | solution.py:24
  253.8 5.7 %collective-permute-done.22 = f32[3,512]{1,0:T(4,128)S(1)} collective-permute-done((f32[3,512]{1,0:T(4,128)S(1)}, f32[3,512]{1,0:T(4,128)S(1)}, u32[]{:S(2)}, u32[]{:S(2)}) %collective-permute-start.22) | collective-permute-done | bytes 6176 | tf_op jit(solution)/shard_map/ppermute | solution.py:24
  261.6 4.2 %collective-permute-done.23 = f32[3,512]{1,0:T(4,128)S(1)} collective-permute-done((f32[3,512]{1,0:T(4,128)S(1)}, f32[3,512]{1,0:T(4,128)S(1)}, u32[]{:S(2)}, u32[]{:S(2)}) %collective-permute-start.23) | collective-permute-done | bytes 6176 | tf_op jit(solution)/shard_map/ppermute | solution.py:24
  265.8 5.6 %psum.7 = f32[3,512]{1,0:T(4,128)} all-reduce(f32[3,512]{1,0:T(4,128)S(1)} %fusion.5), channel_id=1, replica_groups=mesh['slab'=16,'head'=2] {'head'}, use_global_device_ids=true, to_apply=%region_0.1 | all-reduce | flops 1536 | bytes 12288 | tf_op jit(solution)/shard_map/psum | solution.py:305
  271.4 2.6 add_convert_fusion.3
  274.0 2.2 add_convert_fusion
  276.2 1.5 pad_maximum_fusion
  (95 shorter events, 16.0 us)
Async XLA Ops:
  3.7 18.5 %collective-permute-start.4 = (bf16[512,1024]{1,0:T(8,128)(2,1)}, bf16[512,1024]{1,0:T(8,128)(2,1)}, u32[]{:S(2)}, u32[]{:S(2)}) collective-permute-start(bf16[512,1024]{1,0:T(8,128)(2,1)} %get-tuple-element.44.rest_2_), channel_id=1, source_target_pairs={{30,0},{0,2},{2,4},{4,6},{6,8},{8,10},{10,12},{12,14},{14,16},{16,... | collective-permute-start | bytes 3145736 | tf_op jit(solution)/shard_map/ppermute | solution.py:24
  4.2 37.2 %collective-permute-start.6 = (bf16[512,1024]{1,0:T(8,128)(2,1)}, bf16[512,1024]{1,0:T(8,128)(2,1)}, u32[]{:S(2)}, u32[]{:S(2)}) collective-permute-start(bf16[512,1024]{1,0:T(8,128)(2,1)} %get-tuple-element.44.rest_2_), channel_id=1, source_target_pairs={{2,0},{4,2},{6,4},{8,6},{10,8},{12,10},{14,12},{16,14},{18,16},{20... | collective-permute-start | bytes 3145736 | tf_op jit(solution)/shard_map/ppermute | solution.py:24
  9.2 72.9 %collective-permute-start.10 = (bf16[512,1024]{1,0:T(8,128)(2,1)}, bf16[512,1024]{1,0:T(8,128)(2,1)}, u32[]{:S(2)}, u32[]{:S(2)}) collective-permute-start(bf16[512,1024]{1,0:T(8,128)(2,1)} %get-tuple-element.45.rest_2_), channel_id=1, source_target_pairs={{2,0},{4,2},{6,4},{8,6},{10,8},{12,10},{14,12},{16,14},{18,16},{20... | collective-permute-start | bytes 3145736 | tf_op jit(solution)/shard_map/ppermute | solution.py:24
  9.9 73.7 %collective-permute-start.8 = (bf16[512,1024]{1,0:T(8,128)(2,1)}, bf16[512,1024]{1,0:T(8,128)(2,1)}, u32[]{:S(2)}, u32[]{:S(2)}) collective-permute-start(bf16[512,1024]{1,0:T(8,128)(2,1)} %get-tuple-element.45.rest_2_), channel_id=1, source_target_pairs={{30,0},{0,2},{2,4},{4,6},{6,8},{8,10},{10,12},{12,14},{14,16},{16,... | collective-permute-start | bytes 3145736 | tf_op jit(solution)/shard_map/ppermute | solution.py:24
  10.6 35.7 %collective-permute-start = (f32[4,512]{1,0:T(4,128)S(1)}, f32[4,512]{1,0:T(4,128)S(1)}, u32[]{:S(2)}, u32[]{:S(2)}) collective-permute-start(f32[4,512]{1,0:T(4,128)S(1)} %pad_maximum_fusion.1), channel_id=1, source_target_pairs={{28,0},{30,2},{0,4},{2,6},{4,8},{6,10},{8,12},{10,14},{12,16},{14,... | collective-permute-start | bytes 24584 | tf_op jit(solution)/shard_map/ppermute | solution.py:24
  22.2 63.0 %collective-permute-start.5 = (bf16[512,1024]{1,0:T(8,128)(2,1)}, bf16[512,1024]{1,0:T(8,128)(2,1)}, u32[]{:S(2)}, u32[]{:S(2)}) collective-permute-start(bf16[512,1024]{1,0:T(8,128)(2,1)} %collective-permute-done.4.rest_1_), channel_id=1, source_target_pairs={{30,0},{0,2},{2,4},{4,6},{6,8},{8,10},{10,12},{12,14},{14,16},{16,... | collective-permute-start | bytes 3145736 | tf_op jit(solution)/shard_map/ppermute | solution.py:24
  41.5 43.8 %collective-permute-start.7 = (bf16[512,1024]{1,0:T(8,128)(2,1)}, bf16[512,1024]{1,0:T(8,128)(2,1)}, u32[]{:S(2)}, u32[]{:S(2)}) collective-permute-start(bf16[512,1024]{1,0:T(8,128)(2,1)} %collective-permute-done.6.rest_3_), channel_id=1, source_target_pairs={{2,0},{4,2},{6,4},{8,6},{10,8},{12,10},{14,12},{16,14},{18,16},{20... | collective-permute-start | bytes 3145736 | tf_op jit(solution)/shard_map/ppermute | solution.py:24
  43.1 20.8 %copy-start.15 = (f32[4]{0:T(128)S(1)}, f32[4]{0:T(128)}, u32[]{:S(2)}) copy-start(f32[4]{0:T(128)} %constant.19.clone) | copy-start | bytes 52
  43.1 27.4 %copy-start.14 = (f32[4]{0:T(128)S(1)}, f32[4]{0:T(128)}, u32[]{:S(2)}) copy-start(f32[4]{0:T(128)} %constant.20.clone) | copy-start | bytes 52
  43.1 40.5 %copy-start.13 = (f32[4]{0:T(128)S(1)}, f32[4]{0:T(128)}, u32[]{:S(2)}) copy-start(f32[4]{0:T(128)} %constant.22.clone) | copy-start | bytes 52
  43.1 40.6 %copy-start.12 = (f32[4]{0:T(128)S(1)}, f32[4]{0:T(128)}, u32[]{:S(2)}) copy-start(f32[4]{0:T(128)} %constant.23.clone) | copy-start | bytes 52
  46.3 24.2 %collective-permute-start.1 = (f32[4,512]{1,0:T(4,128)S(1)}, f32[4,512]{1,0:T(4,128)S(1)}, u32[]{:S(2)}, u32[]{:S(2)}) collective-permute-start(f32[4,512]{1,0:T(4,128)S(1)} %pad_maximum_fusion.1), channel_id=1, source_target_pairs={{30,0},{0,2},{2,4},{4,6},{6,8},{8,10},{10,12},{12,14},{14,16},{16,... | collective-permute-start | bytes 24584 | tf_op jit(solution)/shard_map/ppermute | solution.py:24
  70.5 5.5 %collective-permute-start.2 = (f32[4,512]{1,0:T(4,128)S(1)}, f32[4,512]{1,0:T(4,128)S(1)}, u32[]{:S(2)}, u32[]{:S(2)}) collective-permute-start(f32[4,512]{1,0:T(4,128)S(1)} %pad_maximum_fusion.1), channel_id=1, source_target_pairs={{2,0},{4,2},{6,4},{8,6},{10,8},{12,10},{14,12},{16,14},{18,16},{20... | collective-permute-start | bytes 24584 | tf_op jit(solution)/shard_map/ppermute | solution.py:24
  76.0 7.6 %collective-permute-start.3 = (f32[4,512]{1,0:T(4,128)S(1)}, f32[4,512]{1,0:T(4,128)S(1)}, u32[]{:S(2)}, u32[]{:S(2)}) collective-permute-start(f32[4,512]{1,0:T(4,128)S(1)} %pad_maximum_fusion.1), channel_id=1, source_target_pairs={{4,0},{6,2},{8,4},{10,6},{12,8},{14,10},{16,12},{18,14},{20,16},{2... | collective-permute-start | bytes 24584 | tf_op jit(solution)/shard_map/ppermute | solution.py:24
  82.1 54.4 %collective-permute-start.11 = (bf16[512,1024]{1,0:T(8,128)(2,1)}, bf16[512,1024]{1,0:T(8,128)(2,1)S(1)}, u32[]{:S(2)}, u32[]{:S(2)}) collective-permute-start(bf16[512,1024]{1,0:T(8,128)(2,1)} %collective-permute-done.10.rest_3_), channel_id=1, source_target_pairs={{2,0},{4,2},{6,4},{8,6},{10,8},{12,10},{14,12},{16,14},{18,16},{20... | collective-permute-start | bytes 3145736 | tf_op jit(solution)/shard_map/ppermute | solution.py:24
  83.5 52.9 %collective-permute-start.9 = (bf16[512,1024]{1,0:T(8,128)(2,1)}, bf16[512,1024]{1,0:T(8,128)(2,1)}, u32[]{:S(2)}, u32[]{:S(2)}) collective-permute-start(bf16[512,1024]{1,0:T(8,128)(2,1)} %collective-permute-done.8.rest_1_), channel_id=1, source_target_pairs={{30,0},{0,2},{2,4},{4,6},{6,8},{8,10},{10,12},{12,14},{14,16},{16,... | collective-permute-start | bytes 3145736 | tf_op jit(solution)/shard_map/ppermute | solution.py:24
  131.7 56.8 %collective-permute-start.12 = (bf16[512,1024]{1,0:T(8,128)(2,1)}, bf16[512,1024]{1,0:T(8,128)(2,1)S(1)}, u32[]{:S(2)}, u32[]{:S(2)}) collective-permute-start(bf16[512,1024]{1,0:T(8,128)(2,1)} %get-tuple-element.22), channel_id=1, source_target_pairs={{30,0},{0,2},{2,4},{4,6},{6,8},{8,10},{10,12},{12,14},{14,16},{16,... | collective-permute-start | bytes 3145736 | tf_op jit(solution)/shard_map/ppermute | solution.py:24
  131.8 59.4 %collective-permute-start.14 = (bf16[512,1024]{1,0:T(8,128)(2,1)}, bf16[512,1024]{1,0:T(8,128)(2,1)S(1)}, u32[]{:S(2)}, u32[]{:S(2)}) collective-permute-start(bf16[512,1024]{1,0:T(8,128)(2,1)} %get-tuple-element.24), channel_id=1, source_target_pairs={{2,0},{4,2},{6,4},{8,6},{10,8},{12,10},{14,12},{16,14},{18,16},{20... | collective-permute-start | bytes 3145736 | tf_op jit(solution)/shard_map/ppermute | solution.py:24
  137.5 52.0 %copy-start.3 = (bf16[512,1024]{1,0:T(8,128)(2,1)S(1)}, bf16[512,1024]{1,0:T(8,128)(2,1)}, u32[]{:S(2)}) copy-start(bf16[512,1024]{1,0:T(8,128)(2,1)} %get-tuple-element.23) | copy-start | bytes 3145732
  184.0 17.3 %collective-permute-start.16 = (bf16[512,1024]{1,0:T(8,128)(2,1)}, bf16[512,1024]{1,0:T(8,128)(2,1)S(1)}, u32[]{:S(2)}, u32[]{:S(2)}) collective-permute-start(bf16[512,1024]{1,0:T(8,128)(2,1)} %get-tuple-element.27), channel_id=1, source_target_pairs={{30,0},{0,2},{2,4},{4,6},{6,8},{8,10},{10,12},{12,14},{14,16},{16,... | collective-permute-start | bytes 3145736 | tf_op jit(solution)/shard_map/ppermute | solution.py:24
  184.0 33.2 %collective-permute-start.18 = (bf16[512,1024]{1,0:T(8,128)(2,1)}, bf16[512,1024]{1,0:T(8,128)(2,1)S(1)}, u32[]{:S(2)}, u32[]{:S(2)}) collective-permute-start(bf16[512,1024]{1,0:T(8,128)(2,1)} %get-tuple-element.29), channel_id=1, source_target_pairs={{2,0},{4,2},{6,4},{8,6},{10,8},{12,10},{14,12},{16,14},{18,16},{20... | collective-permute-start | bytes 3145736 | tf_op jit(solution)/shard_map/ppermute | solution.py:24
  191.1 80.3 %collective-permute-start.13 = (bf16[512,1024]{1,0:T(8,128)(2,1)S(1)}, bf16[512,1024]{1,0:T(8,128)(2,1)}, u32[]{:S(2)}, u32[]{:S(2)}) collective-permute-start(bf16[512,1024]{1,0:T(8,128)(2,1)S(1)} %add_convert_fusion.5), channel_id=1, source_target_pairs={{30,0},{0,2},{2,4},{4,6},{6,8},{8,10},{10,12},{12,14},{14,16},{16,... | collective-permute-start | bytes 3145736 | tf_op jit(solution)/shard_map/ppermute | solution.py:24
  191.6 25.7 %copy-start.4 = (bf16[512,1024]{1,0:T(8,128)(2,1)S(1)}, bf16[512,1024]{1,0:T(8,128)(2,1)}, u32[]{:S(2)}) copy-start(bf16[512,1024]{1,0:T(8,128)(2,1)} %get-tuple-element.30) | copy-start | bytes 3145732
  191.6 79.8 %collective-permute-start.15 = (bf16[512,1024]{1,0:T(8,128)(2,1)S(1)}, bf16[512,1024]{1,0:T(8,128)(2,1)}, u32[]{:S(2)}, u32[]{:S(2)}) collective-permute-start(bf16[512,1024]{1,0:T(8,128)(2,1)S(1)} %add_convert_fusion.4), channel_id=1, source_target_pairs={{2,0},{4,2},{6,4},{8,6},{10,8},{12,10},{14,12},{16,14},{18,16},{20... | collective-permute-start | bytes 3145736 | tf_op jit(solution)/shard_map/ppermute | solution.py:24
  202.6 71.4 %collective-permute-start.17 = (bf16[512,1024]{1,0:T(8,128)(2,1)}, bf16[512,1024]{1,0:T(8,128)(2,1)}, u32[]{:S(2)}, u32[]{:S(2)}) collective-permute-start(bf16[512,1024]{1,0:T(8,128)(2,1)} %add_convert_fusion.2), channel_id=1, source_target_pairs={{30,0},{0,2},{2,4},{4,6},{6,8},{8,10},{10,12},{12,14},{14,16},{16,... | collective-permute-start | bytes 3145736 | tf_op jit(solution)/shard_map/ppermute | solution.py:24
  218.6 55.4 %collective-permute-start.19 = (bf16[512,1024]{1,0:T(8,128)(2,1)}, bf16[512,1024]{1,0:T(8,128)(2,1)}, u32[]{:S(2)}, u32[]{:S(2)}) collective-permute-start(bf16[512,1024]{1,0:T(8,128)(2,1)} %add_convert_fusion.1), channel_id=1, source_target_pairs={{2,0},{4,2},{6,4},{8,6},{10,8},{12,10},{14,12},{16,14},{18,16},{20... | collective-permute-start | bytes 3145736 | tf_op jit(solution)/shard_map/ppermute | solution.py:24
  218.9 46.9 %copy-start.9 = (f32[8,512]{1,0:T(8,128)S(1)}, f32[8,512]{1,0:T(8,128)}, u32[]{:S(2)}) copy-start(f32[8,512]{1,0:T(8,128)} %get-tuple-element.31) | copy-start | bytes 49156
  218.9 46.9 %copy-start.10 = (f32[8,512]{1,0:T(8,128)S(1)}, f32[8,512]{1,0:T(8,128)}, u32[]{:S(2)}) copy-start(f32[8,512]{1,0:T(8,128)} %get-tuple-element.32) | copy-start | bytes 49156
  219.0 33.3 %collective-permute-start.20 = (f32[3,512]{1,0:T(4,128)S(1)}, f32[3,512]{1,0:T(4,128)S(1)}, u32[]{:S(2)}, u32[]{:S(2)}) collective-permute-start(f32[3,512]{1,0:T(4,128)S(1)} %bitcast.43), channel_id=1, source_target_pairs={{4,0},{6,2},{8,4},{10,6},{12,8},{14,10},{16,12},{18,14},{20,16},{2... | collective-permute-start | bytes 18440 | tf_op jit(solution)/shard_map/ppermute | solution.py:24
  252.3 1.4 collective-permute-start.21
  253.7 5.8 %collective-permute-start.22 = (f32[3,512]{1,0:T(4,128)S(1)}, f32[3,512]{1,0:T(4,128)S(1)}, u32[]{:S(2)}, u32[]{:S(2)}) collective-permute-start(f32[3,512]{1,0:T(4,128)S(1)} %bitcast.42), channel_id=1, source_target_pairs={{30,0},{0,2},{2,4},{4,6},{6,8},{8,10},{10,12},{12,14},{14,16},{16,... | collective-permute-start | bytes 18440 | tf_op jit(solution)/shard_map/ppermute | solution.py:24
  259.4 6.3 %collective-permute-start.23 = (f32[3,512]{1,0:T(4,128)S(1)}, f32[3,512]{1,0:T(4,128)S(1)}, u32[]{:S(2)}, u32[]{:S(2)}) collective-permute-start(f32[3,512]{1,0:T(4,128)S(1)} %bitcast.40), channel_id=1, source_target_pairs={{28,0},{30,2},{0,4},{2,6},{4,8},{6,10},{8,12},{10,14},{12,16},{14,... | collective-permute-start | bytes 18440 | tf_op jit(solution)/shard_map/ppermute | solution.py:24
  (9 other events, 67.6 us)

commit v2 on v1

--- a/solution.py
+++ b/solution.py
@@ -11,17 +11,47 @@
 VEC = 32
 WIDTH = 2 * HEAD_DIM + 4 * VEC
 COT = HEAD_DIM + 3 * VEC
-OFFSETS = (-2, -1, 0, 1, 2)
+VIEWS = 5
 FAR = 1e6
 FLOOR = -1e4
 CHUNK = 256
-GROUPS = 2
-
-
-def passed_along(block, axis, distance):
-    count = lax.axis_size(axis)
-    route = [((i - distance) % count, i) for i in range(count)]
+GROUPS = 4
+
+
+def routed(block, axis, target):
+    route = [(i, target(i) % lax.axis_size(axis)) for i in range(lax.axis_size(axis))]
     return lax.ppermute(block, axis, route)
+
+
+def across_pairs(block):
+    return routed(block, "slab", lambda i: i ^ 2)
+
+
+def along_line(block, sign):
+    return routed(block, "slab", lambda i: i + (sign if i & 2 == 0 else -sign) * 4)
+
+
+def across_cores(block):
+    return routed(block, "slab", lambda i: i ^ 1)
+
+
+def fetched_views(block, near):
+    far_one = across_pairs(block)
+    far_two = along_line(far_one, 1)
+    next_one = across_cores(block)
+    next_two = across_cores(jnp.where(near, far_one, far_two))
+    return [block, far_one, far_two, next_one, next_two]
+
+
+def returned_terms(terms, near, dtype):
+    f32 = jnp.float32
+    own, far_one, far_two, next_one, next_two = terms
+    swapped = across_cores(next_two).astype(f32)
+    far_two = far_two.astype(f32) + jnp.where(near, 0.0, swapped)
+    far_one = far_one.astype(f32) + jnp.where(near, swapped, 0.0)
+    far_one = far_one + along_line(far_two.astype(dtype), -1).astype(f32)
+    own = own.astype(f32) + across_cores(next_one).astype(f32)
+    return own + across_pairs(far_one.astype(dtype)).astype(f32)
 
 
 def dot_nt(a, b):
@@ -46,7 +76,7 @@
 
 
 def kernel(gamma_ref, q_ref, c_ref, ct_ref, qc_ref, kc_ref, *rest):
-    views = len(OFFSETS)
+    views = VIEWS
     kv_refs = rest[:views]
     t_refs = rest[views : 2 * views]
     dq_ref, kp_ref, qp_ref = rest[2 * views : 2 * views + 3]
@@ -186,7 +216,7 @@
 
 def head_group(gamma, q, cot, cot_t, query_coords, key_coords, blocks):
     heads, rows, _ = q.shape
-    views = len(OFFSETS)
+    views = VIEWS
     keys = views * rows
     f32 = jnp.float32
     per_head = lambda h: (h, 0, 0)
@@ -247,19 +277,17 @@
     bf16 = jnp.bfloat16
     validity = (jnp.arange(rows, dtype=jnp.int32) < counts[0]).astype(f32)
     coords = jnp.concatenate([positions, validity[None, :]], axis=0)
-    coords_at = {0: coords}
-    for o in (1, -1, 2, -2):
-        coords_at[o] = passed_along(coords, "slab", -o)
-
-    pieces = [key_values[:, g * size * WIDTH : (g + 1) * size * WIDTH] for g in range(groups)]
-    fetched = []
-    for g in range(groups):
-        blocks = {0: pieces[g]}
-        for o in (1, -1):
-            blocks[o] = passed_along(blocks[0], "slab", -o)
-        for o in (1, -1):
-            blocks[2 * o] = passed_along(blocks[o], "slab", -o)
-        fetched.append(blocks)
+    place = lax.axis_index("slab")
+    core, side = place % 2, place // 2 % 2
+    near = core == side
+    far_step = jnp.where(side == 0, 2.0, -2.0).astype(f32)
+    near_step = jnp.where(core == 0, 1.0, -1.0).astype(f32)
+    shifts = [jnp.zeros((), f32), far_step, -far_step, near_step, -near_step]
+    coord_views = fetched_views(coords, near)
+    fetched = [
+        fetched_views(key_values[:, g * size * WIDTH : (g + 1) * size * WIDTH], near)
+        for g in range(groups)
+    ]
 
     q = queries.reshape(rows, heads, HEAD_DIM).transpose(1, 0, 2) * bf16(0.125)
     q = jnp.pad(q, ((0, 0), (0, 0), (0, WIDTH - HEAD_DIM)))
@@ -273,8 +301,9 @@
     cot_t = cot[:, :, 2 * HEAD_DIM : 2 * HEAD_DIM + 3 * VEC].transpose(0, 2, 1)
 
     query_coords = jnp.pad(coords, ((0, 4), (0, 0)))
+    first_row = jnp.array([1, 0, 0, 0], f32)[:, None]
     key_coords = jnp.concatenate(
-        [coords_at[o] + jnp.array([o, 0, 0, 0], f32)[:, None] for o in OFFSETS], axis=1
+        [view + shift * first_row for view, shift in zip(coord_views, shifts)], axis=1
     ).T
 
     dq_parts = []
@@ -284,24 +313,15 @@
     for g in range(groups):
         part = slice(g * size, (g + 1) * size)
         out = head_group(
-            gamma[part], q[part], cot[part], cot_t[part], query_coords, key_coords,
-            [fetched[g][o] for o in OFFSETS],
+            gamma[part], q[part], cot[part], cot_t[part], query_coords, key_coords, fetched[g]
         )
-        terms = dict(zip(OFFSETS, out[: len(OFFSETS)]))
         dq_parts.append(out[-3])
         key_pos = key_pos + out[-2]
         query_pos = query_pos + out[-1][:3]
-        collected = terms[0].astype(f32)
-        for o in (1, -1):
-            moving = passed_along(terms[2 * o], "slab", o)
-            moving = (moving.astype(f32) + terms[o].astype(f32)).astype(bf16)
-            collected = collected + passed_along(moving, "slab", o).astype(f32)
-        kv_parts.append(collected.astype(bf16))
-
-    key_pos = key_pos.T[:3].reshape(3, len(OFFSETS), rows)
-    total = query_pos
-    for n, o in enumerate(OFFSETS):
-        total = total + (key_pos[:, n] if o == 0 else passed_along(key_pos[:, n], "slab", o))
+        kv_parts.append(returned_terms(out[:VIEWS], near, bf16).astype(bf16))
+
+    key_pos = key_pos.T[:3].reshape(3, VIEWS, rows)
+    total = query_pos + returned_terms([key_pos[:, n] for n in range(VIEWS)], near, f32)
     position_grads = lax.psum(total, "head")
     query_grads = jnp.concatenate(dq_parts, axis=0).T
     return (query_grads, jnp.concatenate(kv_parts, axis=1), position_grads)

time: 278 us -> 313 us (1.13); the launches traced: 278 us -> 308 us
  waiting for transfers between devices: 47.8 us -> 108 us
  starting transfers between devices: 94.4 us -> 37.4 us
  Pallas kernels: 92.9 us -> 121 us
    ppermute x24 -> x40, waiting for transfers between devices: 47.8 us -> 108 us  [routed(): return lax.ppermute(block, axis, route)]
    ppermute x24 -> x40, starting transfers between devices: 94.4 us -> 37.4 us  [routed(): return lax.ppermute(block, axis, route)]
    pallas_call x2 -> x4, Pallas kernels: 92.9 us -> 121 us  [head_group(): pl.pallas_call(kernel, grid=(heads,), in_specs=[pl.BlockSpec(memory_space...]
    convert_element_type x6 -> x12, other arithmetic: 9.51 us -> 5.58 us  [the longest x4 4.05 us: per_device(): kv_parts.append(returned_terms(out[:VIEWS], near, bf16).astype(bf16))]
    select_n x0 -> x5, other arithmetic: none -> 3.21 us  [fetched_views(): next_two = across_cores(jnp.where(near, far_one, far_two))]
  transfers between devices with their start and end apart: 24 -> 40, of which waited for: 8 -> 19; matrix products, arithmetic and copies ran while one was open for 10% -> 9% of each run, Pallas kernels for 33% -> 29%
where the time goes in v2:
time: 313 us; the launch traced here: 308 us
  Pallas kernels  121 us (39%)
  waiting for transfers between devices  108 us (35%)
  starting transfers between devices  37.4 us (12%)
  local copies, waits for them, and re-layouts  20.7 us (7%)
  other arithmetic  13.7 us (4%)
  blocking collectives  5.59 us (2%)
    pallas_call x4, Pallas kernels, head_group(): pl.pallas_call(kernel, grid=(heads,), in_specs=[pl.BlockSpec(memory_space...  121 us
    ppermute x40, waiting for transfers between devices, routed(): return lax.ppermute(block, axis, route)  108 us
    ppermute x40, starting transfers between devices, routed(): return lax.ppermute(block, axis, route)  37.4 us
  transfers between devices with their start and end apart: 40, of which 19 were waited for; matrix products, arithmetic and copies ran while one was open for 9% of the time, Pallas kernels for 29%

profile of v2, /device:TPU:0, one launch (start us, length us, event | category | flops | bytes accessed | tf_op | source)
XLA Modules:
  0.0 308.5 jit_solution(11650185092647232390)
XLA Ops:
  2.0 3.1 collective-permute-start
  5.1 2.9 fusion.28
  8.1 1.9 collective-permute-start.8
  23.0 2.0 collective-permute-start.1
  25.1 3.6 %collective-permute-done.1 = f32[4,512]{1,0:T(4,128)S(1)} collective-permute-done((f32[4,512]{1,0:T(4,128)S(1)}, f32[4,512]{1,0:T(4,128)S(1)}, u32[]{:S(2)}, u32[]{:S(2)}) %collective-permute-start.1) | collective-permute-done | bytes 8224 | tf_op jit(solution)/shard_map/ppermute | solution.py:23
  30.3 4.1 %collective-permute-done.8.rest_1_ = bf16[512,512]{1,0:T(8,128)(2,1)} collective-permute-done((bf16[512,512]{1,0:T(8,128)(2,1)}, bf16[512,512]{1,0:T(8,128)(2,1)}, u32[]{:S(2)}, u32[]{:S(2)}) %collective-permute-start.8) | collective-permute-done | bytes 524320 | tf_op jit(solution)/shard_map/ppermute | solution.py:23
  37.6 7.9 %collective-permute-done.16.rest_1_ = bf16[512,512]{1,0:T(8,128)(2,1)S(1)} collective-permute-done((bf16[512,512]{1,0:T(8,128)(2,1)}, bf16[512,512]{1,0:T(8,128)(2,1)S(1)}, u32[]{:S(2)}, u32[]{:S(2)}) %collective-permute-start.16) | collective-permute-done | bytes 524320 | tf_op jit(solution)/shard_map/ppermute | solution.py:23
  48.3 8.0 %collective-permute-done.12.rest_1_ = bf16[512,512]{1,0:T(8,128)(2,1)S(1)} collective-permute-done((bf16[512,512]{1,0:T(8,128)(2,1)}, bf16[512,512]{1,0:T(8,128)(2,1)S(1)}, u32[]{:S(2)}, u32[]{:S(2)}) %collective-permute-start.12) | collective-permute-done | bytes 524320 | tf_op jit(solution)/shard_map/ppermute | solution.py:23
  56.3 1.9 collective-permute-done.9.rest_2_
  58.4 1.9 broadcast_select_fusion.2
  60.3 9.1 %collective-permute-done.17.rest_2_ = bf16[512,512]{1,0:T(8,128)(2,1)S(1)} collective-permute-done((bf16[512,512]{1,0:T(8,128)(2,1)S(1)}, bf16[512,512]{1,0:T(8,128)(2,1)S(1)}, u32[]{:S(2)}, u32[]{:S(2)}) %collective-permute-start.17) | collective-permute-done | bytes 524320 | tf_op jit(solution)/shard_map/ppermute | solution.py:23
  69.5 8.7 %collective-permute-done.13.rest_2_ = bf16[512,512]{1,0:T(8,128)(2,1)S(1)} collective-permute-done((bf16[512,512]{1,0:T(8,128)(2,1)S(1)}, bf16[512,512]{1,0:T(8,128)(2,1)S(1)}, u32[]{:S(2)}, u32[]{:S(2)}) %collective-permute-start.13) | collective-permute-done | bytes 524320 | tf_op jit(solution)/shard_map/ppermute | solution.py:23
  79.7 30.0 %pairs.4 = (bf16[512,512]{1,0:T(8,128)(2,1)}, bf16[512,512]{1,0:T(8,128)(2,1)}, bf16[512,512]{1,0:T(8,128)(2,1)}, bf16[512,512]{1,0:T(8,128)(2,1)}, bf16[512,512...) custom-call(f32[2]{0:T(128)} %get-tuple-element.104.gamma_ref, ...), custom_call_target="tpu_custom_call" | custom-call | flops 3932160000 | bytes 5242880 | tf_op jit(solution)/shard_map/pairs/pallas_call | solution.py:225
  109.9 30.4 %pairs.5 = (bf16[512,512]{1,0:T(8,128)(2,1)}, bf16[512,512]{1,0:T(8,128)(2,1)}, bf16[512,512]{1,0:T(8,128)(2,1)}, bf16[512,512]{1,0:T(8,128)(2,1)}, bf16[512,512...) custom-call(f32[2]{0:T(128)} %get-tuple-element.105.gamma_ref, ...), custom_call_target="tpu_custom_call" | custom-call | flops 3932160000 | bytes 5242880 | tf_op jit(solution)/shard_map/pairs/pallas_call | solution.py:225
  141.3 30.5 %pairs.6 = (bf16[512,512]{1,0:T(8,128)(2,1)}, bf16[512,512]{1,0:T(8,128)(2,1)}, bf16[512,512]{1,0:T(8,128)(2,1)}, bf16[512,512]{1,0:T(8,128)(2,1)}, bf16[512,512...) custom-call(f32[2]{0:T(128)} %get-tuple-element.107.gamma_ref, ...), custom_call_target="tpu_custom_call" | custom-call | flops 3932160000 | bytes 5242880 | tf_op jit(solution)/shard_map/pairs/pallas_call | solution.py:225
  172.6 30.4 %pairs.7 = (bf16[512,512]{1,0:T(8,128)(2,1)}, bf16[512,512]{1,0:T(8,128)(2,1)}, bf16[512,512]{1,0:T(8,128)(2,1)}, bf16[512,512]{1,0:T(8,128)(2,1)}, bf16[512,512...) custom-call(f32[2]{0:T(128)} %get-tuple-element.106.gamma_ref, ...), custom_call_target="tpu_custom_call" | custom-call | flops 3932160000 | bytes 5242880 | tf_op jit(solution)/shard_map/pairs/pallas_call | solution.py:225
  206.2 1.7 collective-permute-start.38
  209.9 1.8 collective-permute-start.39
  213.6 5.6 %psum.7 = f32[3,512]{1,0:T(4,128)} all-reduce(f32[3,512]{1,0:T(4,128)S(1)} %fusion.26), channel_id=1, replica_groups=mesh['slab'=16,'head'=2] {'head'}, use_global_device_ids=true, to_apply=%region_0.1 | all-reduce | flops 1536 | bytes 12288 | tf_op jit(solution)/shard_map/psum | solution.py:325
  221.3 3.5 %collective-permute-start.34 = (bf16[512,512]{1,0:T(8,128)(2,1)S(1)}, bf16[512,512]{1,0:T(8,128)(2,1)S(1)}, u32[]{:S(2)}, u32[]{:S(2)}) collective-permute-start(bf16[512,512]{1,0:T(8,128)(2,1)S(1)} %fusion.20), channel_id=1, source_target_pairs={{0,24},{2,26},{4,12},{6,14},{8,0},{10,2},{12,20},{14,22},{16,8},{1... | collective-permute-start | bytes 1572872 | tf_op jit(solution)/shard_map/ppermute | solution.py:23
  226.0 11.2 %collective-permute-done.34 = bf16[512,512]{1,0:T(8,128)(2,1)S(1)} collective-permute-done((bf16[512,512]{1,0:T(8,128)(2,1)S(1)}, bf16[512,512]{1,0:T(8,128)(2,1)S(1)}, u32[]{:S(2)}, u32[]{:S(2)}) %collective-permute-start.34) | collective-permute-done | bytes 524320 | tf_op jit(solution)/shard_map/ppermute | solution.py:23
  237.2 4.3 %collective-permute-start.26 = (bf16[512,512]{1,0:T(8,128)(2,1)S(1)}, bf16[512,512]{1,0:T(8,128)(2,1)S(1)}, u32[]{:S(2)}, u32[]{:S(2)}) collective-permute-start(bf16[512,512]{1,0:T(8,128)(2,1)S(1)} %fusion.10), channel_id=1, source_target_pairs={{0,24},{2,26},{4,12},{6,14},{8,0},{10,2},{12,20},{14,22},{16,8},{1... | collective-permute-start | bytes 1572872 | tf_op jit(solution)/shard_map/ppermute | solution.py:23
  241.7 6.7 %collective-permute-done.30 = bf16[512,512]{1,0:T(8,128)(2,1)S(1)} collective-permute-done((bf16[512,512]{1,0:T(8,128)(2,1)S(1)}, bf16[512,512]{1,0:T(8,128)(2,1)S(1)}, u32[]{:S(2)}, u32[]{:S(2)}) %collective-permute-start.30) | collective-permute-done | bytes 524320 | tf_op jit(solution)/shard_map/ppermute | solution.py:23
  248.4 4.3 %collective-permute-start.22 = (bf16[512,512]{1,0:T(8,128)(2,1)S(1)}, bf16[512,512]{1,0:T(8,128)(2,1)S(1)}, u32[]{:S(2)}, u32[]{:S(2)}) collective-permute-start(bf16[512,512]{1,0:T(8,128)(2,1)S(1)} %fusion.5), channel_id=1, source_target_pairs={{0,24},{2,26},{4,12},{6,14},{8,0},{10,2},{12,20},{14,22},{16,8},{1... | collective-permute-start | bytes 1572872 | tf_op jit(solution)/shard_map/ppermute | solution.py:23
  252.9 6.7 %collective-permute-done.26 = bf16[512,512]{1,0:T(8,128)(2,1)S(1)} collective-permute-done((bf16[512,512]{1,0:T(8,128)(2,1)S(1)}, bf16[512,512]{1,0:T(8,128)(2,1)S(1)}, u32[]{:S(2)}, u32[]{:S(2)}) %collective-permute-start.26) | collective-permute-done | bytes 524320 | tf_op jit(solution)/shard_map/ppermute | solution.py:23
  259.6 2.5 collective-permute-start.35
  262.4 7.6 %collective-permute-done.22 = bf16[512,512]{1,0:T(8,128)(2,1)S(1)} collective-permute-done((bf16[512,512]{1,0:T(8,128)(2,1)S(1)}, bf16[512,512]{1,0:T(8,128)(2,1)S(1)}, u32[]{:S(2)}, u32[]{:S(2)}) %collective-permute-start.22) | collective-permute-done | bytes 524320 | tf_op jit(solution)/shard_map/ppermute | solution.py:23
  270.0 2.5 collective-permute-start.31
  276.4 9.0 %collective-permute-done.31 = bf16[512,512]{1,0:T(8,128)(2,1)S(1)} collective-permute-done((bf16[512,512]{1,0:T(8,128)(2,1)S(1)}, bf16[512,512]{1,0:T(8,128)(2,1)S(1)}, u32[]{:S(2)}, u32[]{:S(2)}) %collective-permute-start.31) | collective-permute-done | bytes 524320 | tf_op jit(solution)/shard_map/ppermute | solution.py:23
  286.7 9.9 %collective-permute-done.27 = bf16[512,512]{1,0:T(8,128)(2,1)S(1)} collective-permute-done((bf16[512,512]{1,0:T(8,128)(2,1)S(1)}, bf16[512,512]{1,0:T(8,128)(2,1)S(1)}, u32[]{:S(2)}, u32[]{:S(2)}) %collective-permute-start.27) | collective-permute-done | bytes 524320 | tf_op jit(solution)/shard_map/ppermute | solution.py:23
  297.8 8.6 %collective-permute-done.23 = bf16[512,512]{1,0:T(8,128)(2,1)S(1)} collective-permute-done((bf16[512,512]{1,0:T(8,128)(2,1)S(1)}, bf16[512,512]{1,0:T(8,128)(2,1)S(1)}, u32[]{:S(2)}, u32[]{:S(2)}) %collective-permute-start.23) | collective-permute-done | bytes 524320 | tf_op jit(solution)/shard_map/ppermute | solution.py:23
  306.6 1.6 pad_maximum_fusion
  (187 shorter events, 42.1 us)
Async XLA Ops:
  2.0 21.0 %collective-permute-start = (f32[4,512]{1,0:T(4,128)S(1)}, f32[4,512]{1,0:T(4,128)S(1)}, u32[]{:S(2)}, u32[]{:S(2)}) collective-permute-start(f32[4,512]{1,0:T(4,128)S(1)} %get-tuple-element.77), channel_id=1, source_target_pairs={{0,4},{2,6},{4,0},{6,2},{8,12},{10,14},{12,8},{14,10},{16,20},{18,... | collective-permute-start | bytes 24584 | tf_op jit(solution)/shard_map/ppermute | solution.py:23
  5.1 25.2 %collective-permute-start.2 = (f32[4,512]{1,0:T(4,128)S(1)}, f32[4,512]{1,0:T(4,128)S(1)}, u32[]{:S(2)}, u32[]{:S(2)}) collective-permute-start(f32[4,512]{1,0:T(4,128)S(1)} %get-tuple-element.77), channel_id=1, source_target_pairs={{0,2},{2,0},{4,6},{6,4},{8,10},{10,8},{12,14},{14,12},{16,18},{18,... | collective-permute-start | bytes 24584 | tf_op jit(solution)/shard_map/ppermute | solution.py:23
  8.0 21.9 %collective-permute-start.4 = (bf16[512,512]{1,0:T(8,128)(2,1)}, bf16[512,512]{1,0:T(8,128)(2,1)}, u32[]{:S(2)}, u32[]{:S(2)}) collective-permute-start(bf16[512,512]{1,0:T(8,128)(2,1)} %get-tuple-element.78.rest_0_), channel_id=1, source_target_pairs={{0,4},{2,6},{4,0},{6,2},{8,12},{10,14},{12,8},{14,10},{16,20},{18,... | collective-permute-start | bytes 1572872 | tf_op jit(solution)/shard_map/ppermute | solution.py:23
  8.1 26.3 %collective-permute-start.8 = (bf16[512,512]{1,0:T(8,128)(2,1)}, bf16[512,512]{1,0:T(8,128)(2,1)}, u32[]{:S(2)}, u32[]{:S(2)}) collective-permute-start(bf16[512,512]{1,0:T(8,128)(2,1)} %get-tuple-element.79.rest_0_), channel_id=1, source_target_pairs={{0,4},{2,6},{4,0},{6,2},{8,12},{10,14},{12,8},{14,10},{16,20},{18,... | collective-permute-start | bytes 1572872 | tf_op jit(solution)/shard_map/ppermute | solution.py:23
  10.1 35.5 %collective-permute-start.16 = (bf16[512,512]{1,0:T(8,128)(2,1)}, bf16[512,512]{1,0:T(8,128)(2,1)S(1)}, u32[]{:S(2)}, u32[]{:S(2)}) collective-permute-start(bf16[512,512]{1,0:T(8,128)(2,1)} %get-tuple-element.80.rest_0_), channel_id=1, source_target_pairs={{0,4},{2,6},{4,0},{6,2},{8,12},{10,14},{12,8},{14,10},{16,20},{18,... | collective-permute-start | bytes 1572872 | tf_op jit(solution)/shard_map/ppermute | solution.py:23
  28.7 27.6 %collective-permute-start.12 = (bf16[512,512]{1,0:T(8,128)(2,1)}, bf16[512,512]{1,0:T(8,128)(2,1)S(1)}, u32[]{:S(2)}, u32[]{:S(2)}) collective-permute-start(bf16[512,512]{1,0:T(8,128)(2,1)} %get-tuple-element.81.rest_0_), channel_id=1, source_target_pairs={{0,4},{2,6},{4,0},{6,2},{8,12},{10,14},{12,8},{14,10},{16,20},{18,... | collective-permute-start | bytes 1572872 | tf_op jit(solution)/shard_map/ppermute | solution.py:23
  29.9 17.1 %collective-permute-start.5 = (bf16[512,512]{1,0:T(8,128)(2,1)}, bf16[512,512]{1,0:T(8,128)(2,1)S(1)}, u32[]{:S(2)}, u32[]{:S(2)}) collective-permute-start(bf16[512,512]{1,0:T(8,128)(2,1)} %collective-permute-done.4.rest_1_), channel_id=1, source_target_pairs={{0,8},{2,10},{4,28},{6,30},{8,16},{10,18},{12,4},{14,6},{16,24},{1... | collective-permute-start | bytes 1572872 | tf_op jit(solution)/shard_map/ppermute | solution.py:23
  34.4 23.8 %collective-permute-start.9 = (bf16[512,512]{1,0:T(8,128)(2,1)}, bf16[512,512]{1,0:T(8,128)(2,1)S(1)}, u32[]{:S(2)}, u32[]{:S(2)}) collective-permute-start(bf16[512,512]{1,0:T(8,128)(2,1)} %collective-permute-done.8.rest_1_), channel_id=1, source_target_pairs={{0,8},{2,10},{4,28},{6,30},{8,16},{10,18},{12,4},{14,6},{16,24},{1... | collective-permute-start | bytes 1572872 | tf_op jit(solution)/shard_map/ppermute | solution.py:23
  36.0 42.3 %collective-permute-start.6 = (bf16[512,512]{1,0:T(8,128)(2,1)}, bf16[512,512]{1,0:T(8,128)(2,1)}, u32[]{:S(2)}, u32[]{:S(2)}) collective-permute-start(bf16[512,512]{1,0:T(8,128)(2,1)} %get-tuple-element.78.rest_0_), channel_id=1, source_target_pairs={{0,2},{2,0},{4,6},{6,4},{8,10},{10,8},{12,14},{14,12},{16,18},{18,... | collective-permute-start | bytes 1572872 | tf_op jit(solution)/shard_map/ppermute | solution.py:23
  45.5 64.3 %collective-permute-start.10 = (bf16[512,512]{1,0:T(8,128)(2,1)}, bf16[512,512]{1,0:T(8,128)(2,1)}, u32[]{:S(2)}, u32[]{:S(2)}) collective-permute-start(bf16[512,512]{1,0:T(8,128)(2,1)} %get-tuple-element.79.rest_0_), channel_id=1, source_target_pairs={{0,2},{2,0},{4,6},{6,4},{8,10},{10,8},{12,14},{14,12},{16,18},{18,... | collective-permute-start | bytes 1572872 | tf_op jit(solution)/shard_map/ppermute | solution.py:23
  47.0 22.5 %collective-permute-start.17 = (bf16[512,512]{1,0:T(8,128)(2,1)S(1)}, bf16[512,512]{1,0:T(8,128)(2,1)S(1)}, u32[]{:S(2)}, u32[]{:S(2)}) collective-permute-start(bf16[512,512]{1,0:T(8,128)(2,1)S(1)} %collective-permute-done.16.rest_1_), channel_id=1, source_target_pairs={{0,8},{2,10},{4,28},{6,30},{8,16},{10,18},{12,4},{14,6},{16,24},{1... | collective-permute-start | bytes 1572872 | tf_op jit(solution)/shard_map/ppermute | solution.py:23
  56.3 115.5 %collective-permute-start.18 = (bf16[512,512]{1,0:T(8,128)(2,1)}, bf16[512,512]{1,0:T(8,128)(2,1)}, u32[]{:S(2)}, u32[]{:S(2)}) collective-permute-start(bf16[512,512]{1,0:T(8,128)(2,1)} %get-tuple-element.80.rest_0_), channel_id=1, source_target_pairs={{0,2},{2,0},{4,6},{6,4},{8,10},{10,8},{12,14},{14,12},{16,18},{18,... | collective-permute-start | bytes 1572872 | tf_op jit(solution)/shard_map/ppermute | solution.py:23
  58.2 20.0 %collective-permute-start.13 = (bf16[512,512]{1,0:T(8,128)(2,1)S(1)}, bf16[512,512]{1,0:T(8,128)(2,1)S(1)}, u32[]{:S(2)}, u32[]{:S(2)}) collective-permute-start(bf16[512,512]{1,0:T(8,128)(2,1)S(1)} %collective-permute-done.12.rest_1_), channel_id=1, source_target_pairs={{0,8},{2,10},{4,28},{6,30},{8,16},{10,18},{12,4},{14,6},{16,24},{1... | collective-permute-start | bytes 1572872 | tf_op jit(solution)/shard_map/ppermute | solution.py:23
  69.5 9.5 %collective-permute-start.7 = (bf16[512,512]{1,0:T(8,128)(2,1)S(1)}, bf16[512,512]{1,0:T(8,128)(2,1)S(1)}, u32[]{:S(2)}, u32[]{:S(2)}) collective-permute-start(bf16[512,512]{1,0:T(8,128)(2,1)S(1)} %broadcast_select_fusion.3), channel_id=1, source_target_pairs={{0,2},{2,0},{4,6},{6,4},{8,10},{10,8},{12,14},{14,12},{16,18},{18,... | collective-permute-start | bytes 1572872 | tf_op jit(solution)/shard_map/ppermute | solution.py:23
  78.2 31.6 %collective-permute-start.11 = (bf16[512,512]{1,0:T(8,128)(2,1)}, bf16[512,512]{1,0:T(8,128)(2,1)}, u32[]{:S(2)}, u32[]{:S(2)}) collective-permute-start(bf16[512,512]{1,0:T(8,128)(2,1)} %broadcast_select_fusion.2), channel_id=1, source_target_pairs={{0,2},{2,0},{4,6},{6,4},{8,10},{10,8},{12,14},{14,12},{16,18},{18,... | collective-permute-start | bytes 1572872 | tf_op jit(solution)/shard_map/ppermute | solution.py:23
  78.3 61.9 %collective-permute-start.14 = (bf16[512,512]{1,0:T(8,128)(2,1)}, bf16[512,512]{1,0:T(8,128)(2,1)S(1)}, u32[]{:S(2)}, u32[]{:S(2)}) collective-permute-start(bf16[512,512]{1,0:T(8,128)(2,1)} %get-tuple-element.81.rest_0_), channel_id=1, source_target_pairs={{0,2},{2,0},{4,6},{6,4},{8,10},{10,8},{12,14},{14,12},{16,18},{18,... | collective-permute-start | bytes 1572872 | tf_op jit(solution)/shard_map/ppermute | solution.py:23
  78.9 61.4 %collective-permute-start.15 = (bf16[512,512]{1,0:T(8,128)(2,1)S(1)}, bf16[512,512]{1,0:T(8,128)(2,1)S(1)}, u32[]{:S(2)}, u32[]{:S(2)}) collective-permute-start(bf16[512,512]{1,0:T(8,128)(2,1)S(1)} %broadcast_select_fusion.1), channel_id=1, source_target_pairs={{0,2},{2,0},{4,6},{6,4},{8,10},{10,8},{12,14},{14,12},{16,18},{18,... | collective-permute-start | bytes 1572872 | tf_op jit(solution)/shard_map/ppermute | solution.py:23
  109.8 62.0 %collective-permute-start.19 = (bf16[512,512]{1,0:T(8,128)(2,1)S(1)}, bf16[512,512]{1,0:T(8,128)(2,1)S(1)}, u32[]{:S(2)}, u32[]{:S(2)}) collective-permute-start(bf16[512,512]{1,0:T(8,128)(2,1)S(1)} %broadcast_select_fusion), channel_id=1, source_target_pairs={{0,2},{2,0},{4,6},{6,4},{8,10},{10,8},{12,14},{14,12},{16,18},{18,... | collective-permute-start | bytes 1572872 | tf_op jit(solution)/shard_map/ppermute | solution.py:23
  208.3 10.9 %collective-permute-start.33 = (bf16[512,512]{1,0:T(8,128)(2,1)}, bf16[512,512]{1,0:T(8,128)(2,1)S(1)}, u32[]{:S(2)}, u32[]{:S(2)}) collective-permute-start(bf16[512,512]{1,0:T(8,128)(2,1)} %get-tuple-element.57), channel_id=1, source_target_pairs={{0,2},{2,0},{4,6},{6,4},{8,10},{10,8},{12,14},{14,12},{16,18},{18,... | collective-permute-start | bytes 1572872 | tf_op jit(solution)/shard_map/ppermute | solution.py:23
  208.8 10.6 %collective-permute-start.29 = (bf16[512,512]{1,0:T(8,128)(2,1)}, bf16[512,512]{1,0:T(8,128)(2,1)S(1)}, u32[]{:S(2)}, u32[]{:S(2)}) collective-permute-start(bf16[512,512]{1,0:T(8,128)(2,1)} %get-tuple-element.52), channel_id=1, source_target_pairs={{0,2},{2,0},{4,6},{6,4},{8,10},{10,8},{12,14},{14,12},{16,18},{18,... | collective-permute-start | bytes 1572872 | tf_op jit(solution)/shard_map/ppermute | solution.py:23
  212.9 59.9 %collective-permute-start.32 = (bf16[512,512]{1,0:T(8,128)(2,1)}, bf16[512,512]{1,0:T(8,128)(2,1)}, u32[]{:S(2)}, u32[]{:S(2)}) collective-permute-start(bf16[512,512]{1,0:T(8,128)(2,1)} %get-tuple-element.55), channel_id=1, source_target_pairs={{0,2},{2,0},{4,6},{6,4},{8,10},{10,8},{12,14},{14,12},{16,18},{18,... | collective-permute-start | bytes 1572872 | tf_op jit(solution)/shard_map/ppermute | solution.py:23
  212.9 62.8 %collective-permute-start.28 = (bf16[512,512]{1,0:T(8,128)(2,1)}, bf16[512,512]{1,0:T(8,128)(2,1)}, u32[]{:S(2)}, u32[]{:S(2)}) collective-permute-start(bf16[512,512]{1,0:T(8,128)(2,1)} %get-tuple-element.50), channel_id=1, source_target_pairs={{0,2},{2,0},{4,6},{6,4},{8,10},{10,8},{12,14},{14,12},{16,18},{18,... | collective-permute-start | bytes 1572872 | tf_op jit(solution)/shard_map/ppermute | solution.py:23
  213.5 73.1 %collective-permute-start.24 = (bf16[512,512]{1,0:T(8,128)(2,1)}, bf16[512,512]{1,0:T(8,128)(2,1)}, u32[]{:S(2)}, u32[]{:S(2)}) collective-permute-start(bf16[512,512]{1,0:T(8,128)(2,1)} %get-tuple-element.45), channel_id=1, source_target_pairs={{0,2},{2,0},{4,6},{6,4},{8,10},{10,8},{12,14},{14,12},{16,18},{18,... | collective-permute-start | bytes 1572872 | tf_op jit(solution)/shard_map/ppermute | solution.py:23
  221.3 15.9 %collective-permute-start.34 = (bf16[512,512]{1,0:T(8,128)(2,1)S(1)}, bf16[512,512]{1,0:T(8,128)(2,1)S(1)}, u32[]{:S(2)}, u32[]{:S(2)}) collective-permute-start(bf16[512,512]{1,0:T(8,128)(2,1)S(1)} %fusion.20), channel_id=1, source_target_pairs={{0,24},{2,26},{4,12},{6,14},{8,0},{10,2},{12,20},{14,22},{16,8},{1... | collective-permute-start | bytes 1572872 | tf_op jit(solution)/shard_map/ppermute | solution.py:23
  225.0 23.4 %collective-permute-start.30 = (bf16[512,512]{1,0:T(8,128)(2,1)S(1)}, bf16[512,512]{1,0:T(8,128)(2,1)S(1)}, u32[]{:S(2)}, u32[]{:S(2)}) collective-permute-start(bf16[512,512]{1,0:T(8,128)(2,1)S(1)} %fusion.15), channel_id=1, source_target_pairs={{0,24},{2,26},{4,12},{6,14},{8,0},{10,2},{12,20},{14,22},{16,8},{1... | collective-permute-start | bytes 1572872 | tf_op jit(solution)/shard_map/ppermute | solution.py:23
  237.2 22.5 %collective-permute-start.26 = (bf16[512,512]{1,0:T(8,128)(2,1)S(1)}, bf16[512,512]{1,0:T(8,128)(2,1)S(1)}, u32[]{:S(2)}, u32[]{:S(2)}) collective-permute-start(bf16[512,512]{1,0:T(8,128)(2,1)S(1)} %fusion.10), channel_id=1, source_target_pairs={{0,24},{2,26},{4,12},{6,14},{8,0},{10,2},{12,20},{14,22},{16,8},{1... | collective-permute-start | bytes 1572872 | tf_op jit(solution)/shard_map/ppermute | solution.py:23
  248.4 21.6 %collective-permute-start.22 = (bf16[512,512]{1,0:T(8,128)(2,1)S(1)}, bf16[512,512]{1,0:T(8,128)(2,1)S(1)}, u32[]{:S(2)}, u32[]{:S(2)}) collective-permute-start(bf16[512,512]{1,0:T(8,128)(2,1)S(1)} %fusion.5), channel_id=1, source_target_pairs={{0,24},{2,26},{4,12},{6,14},{8,0},{10,2},{12,20},{14,22},{16,8},{1... | collective-permute-start | bytes 1572872 | tf_op jit(solution)/shard_map/ppermute | solution.py:23
  259.6 13.3 %collective-permute-start.35 = (bf16[512,512]{1,0:T(8,128)(2,1)S(1)}, bf16[512,512]{1,0:T(8,128)(2,1)S(1)}, u32[]{:S(2)}, u32[]{:S(2)}) collective-permute-start(bf16[512,512]{1,0:T(8,128)(2,1)S(1)} %fusion.18), channel_id=1, source_target_pairs={{0,4},{2,6},{4,0},{6,2},{8,12},{10,14},{12,8},{14,10},{16,20},{18,... | collective-permute-start | bytes 1572872 | tf_op jit(solution)/shard_map/ppermute | solution.py:23
  270.0 15.3 %collective-permute-start.31 = (bf16[512,512]{1,0:T(8,128)(2,1)S(1)}, bf16[512,512]{1,0:T(8,128)(2,1)S(1)}, u32[]{:S(2)}, u32[]{:S(2)}) collective-permute-start(bf16[512,512]{1,0:T(8,128)(2,1)S(1)} %fusion.13), channel_id=1, source_target_pairs={{0,4},{2,6},{4,0},{6,2},{8,12},{10,14},{12,8},{14,10},{16,20},{18,... | collective-permute-start | bytes 1572872 | tf_op jit(solution)/shard_map/ppermute | solution.py:23
  272.8 25.0 %collective-permute-start.20 = (bf16[512,512]{1,0:T(8,128)(2,1)S(1)}, bf16[512,512]{1,0:T(8,128)(2,1)S(1)}, u32[]{:S(2)}, u32[]{:S(2)}) collective-permute-start(bf16[512,512]{1,0:T(8,128)(2,1)S(1)} %copy-done.34), channel_id=1, source_target_pairs={{0,2},{2,0},{4,6},{6,4},{8,10},{10,8},{12,14},{14,12},{16,18},{18,... | collective-permute-start | bytes 1572872 | tf_op jit(solution)/shard_map/ppermute | solution.py:23
  272.9 23.7 %collective-permute-start.27 = (bf16[512,512]{1,0:T(8,128)(2,1)S(1)}, bf16[512,512]{1,0:T(8,128)(2,1)S(1)}, u32[]{:S(2)}, u32[]{:S(2)}) collective-permute-start(bf16[512,512]{1,0:T(8,128)(2,1)S(1)} %fusion.8), channel_id=1, source_target_pairs={{0,4},{2,6},{4,0},{6,2},{8,12},{10,14},{12,8},{14,10},{16,20},{18,... | collective-permute-start | bytes 1572872 | tf_op jit(solution)/shard_map/ppermute | solution.py:23
  275.8 30.6 %collective-permute-start.23 = (bf16[512,512]{1,0:T(8,128)(2,1)S(1)}, bf16[512,512]{1,0:T(8,128)(2,1)S(1)}, u32[]{:S(2)}, u32[]{:S(2)}) collective-permute-start(bf16[512,512]{1,0:T(8,128)(2,1)S(1)} %fusion.3), channel_id=1, source_target_pairs={{0,4},{2,6},{4,0},{6,2},{8,12},{10,14},{12,8},{14,10},{16,20},{18,... | collective-permute-start | bytes 1572872 | tf_op jit(solution)/shard_map/ppermute | solution.py:23
  (47 other events, 593.3 us)

commit v3 on v2

--- a/solution.py
+++ b/solution.py
@@ -15,7 +15,7 @@
 FAR = 1e6
 FLOOR = -1e4
 CHUNK = 256
-GROUPS = 4
+GROUPS = 2
 
 
 def routed(block, axis, target):
@@ -260,7 +260,7 @@
             dimension_semantics=("arbitrary",), vmem_limit_bytes=60 * 2**20
         ),
         cost_estimate=pl.CostEstimate(
-            flops=heads * rows * keys * 1500,
+            flops=heads * rows * keys * 10000,
             bytes_accessed=heads * keys * WIDTH * 4,
             transcendentals=heads * rows * keys,
         ),

time: 313 us -> 269 us (0.86); the launches traced: 308 us -> 269 us
  Pallas kernels: 121 us -> 93.2 us
  starting transfers between devices: 37.4 us -> 22.3 us
  other arithmetic: 13.7 us -> 20.4 us
    pallas_call x4 -> x2, Pallas kernels: 121 us -> 93.2 us  [head_group(): pl.pallas_call(kernel, grid=(heads,), in_specs=[pl.BlockSpec(memory_space...]
    ppermute x40 -> x24, starting transfers between devices: 37.4 us -> 22.3 us  [routed(): return lax.ppermute(block, axis, route)]
    convert_element_type x4 -> x2, other arithmetic: 0.9 us -> 4.93 us  [returned_terms(): return own + across_pairs(far_one.astype(dtype)).astype(f32)]
    ppermute x40 -> x24, waiting for transfers between devices: 108 us -> 106 us  [routed(): return lax.ppermute(block, axis, route)]
  transfers between devices with their start and end apart: 40 -> 24, of which waited for: 19 -> 10; matrix products, arithmetic and copies ran while one was open for 9% -> 13% of each run, Pallas kernels for 29% -> 35%
where the time goes in v3:
time: 269 us
  waiting for transfers between devices  106 us (39%)
  Pallas kernels  93.2 us (35%)
  starting transfers between devices  22.3 us (8%)
  other arithmetic  20.4 us (8%)
  local copies, waits for them, and re-layouts  20.2 us (8%)
  blocking collectives  5.59 us (2%)
    ppermute x24, waiting for transfers between devices, routed(): return lax.ppermute(block, axis, route)  106 us
    pallas_call x2, Pallas kernels, head_group(): pl.pallas_call(kernel, grid=(heads,), in_specs=[pl.BlockSpec(memory_space...  93.2 us
    ppermute x24, starting transfers between devices, routed(): return lax.ppermute(block, axis, route)  22.3 us
    psum x1, blocking collectives, per_device(): position_grads = lax.psum(total, 'head')  5.59 us
  transfers between devices with their start and end apart: 24, of which 10 were waited for; matrix products, arithmetic and copies ran while one was open for 13% of the time, Pallas kernels for 35%

profile of v3, /device:TPU:0, one launch (start us, length us, event | category | flops | bytes accessed | tf_op | source)
XLA Modules:
  0.0 268.8 jit_solution(20889995597778362)
XLA Ops:
  2.0 3.0 %collective-permute-start = (f32[4,512]{1,0:T(4,128)S(1)}, f32[4,512]{1,0:T(4,128)S(1)}, u32[]{:S(2)}, u32[]{:S(2)}) collective-permute-start(f32[4,512]{1,0:T(4,128)S(1)} %get-tuple-element.45), channel_id=1, source_target_pairs={{0,4},{2,6},{4,0},{6,2},{8,12},{10,14},{12,8},{14,10},{16,20},{18,... | collective-permute-start | bytes 24584 | tf_op jit(solution)/shard_map/ppermute | solution.py:23
  5.0 3.1 %fusion.18 = (bf16[512,1024]{1,0:T(8,128)(2,1)}, bf16[512,1024]{1,0:T(8,128)(2,1)}) fusion(bf16[512,2048]{1,0:T(8,128)(2,1)} %param.8), kind=kLoop, calls=%fused_computation.55 | loop fusion | bytes 4194304 | tf_op jit(solution)/shard_map/slice | solution.py:288
  8.6 1.7 collective-permute-start.8
  10.3 1.6 copy.34
  16.6 17.8 %collective-permute-done.4.rest_1_ = bf16[512,1024]{1,0:T(8,128)(2,1)} collective-permute-done((bf16[512,1024]{1,0:T(8,128)(2,1)}, bf16[512,1024]{1,0:T(8,128)(2,1)}, u32[]{:S(2)}, u32[]{:S(2)}) %collective-permute-start.4) | collective-permute-done | bytes 1048608 | tf_op jit(solution)/shard_map/ppermute | solution.py:23
  34.4 1.6 collective-permute-start.5
  37.7 1.6 pad_slice_fusion.1
  42.6 1.6 collective-permute-start.1
  44.1 12.3 %collective-permute-done.8.rest_1_ = bf16[512,1024]{1,0:T(8,128)(2,1)} collective-permute-done((bf16[512,1024]{1,0:T(8,128)(2,1)}, bf16[512,1024]{1,0:T(8,128)(2,1)}, u32[]{:S(2)}, u32[]{:S(2)}) %collective-permute-start.8) | collective-permute-done | bytes 1048608 | tf_op jit(solution)/shard_map/ppermute | solution.py:23
  56.4 1.6 collective-permute-start.9
  58.0 2.9 %collective-permute-done.5.rest_2_ = bf16[512,1024]{1,0:T(8,128)(2,1)S(1)} collective-permute-done((bf16[512,1024]{1,0:T(8,128)(2,1)}, bf16[512,1024]{1,0:T(8,128)(2,1)S(1)}, u32[]{:S(2)}, u32[]{:S(2)}) %collective-permute-start.5) | collective-permute-done | bytes 1048608 | tf_op jit(solution)/shard_map/ppermute | solution.py:23
  60.9 1.7 broadcast_select_fusion.1
  63.5 3.5 %collective-permute-done.3 = f32[4,512]{1,0:T(4,128)S(1)} collective-permute-done((f32[4,512]{1,0:T(4,128)S(1)}, f32[4,512]{1,0:T(4,128)S(1)}, u32[]{:S(2)}, u32[]{:S(2)}) %collective-permute-start.3) | collective-permute-done | bytes 8224 | tf_op jit(solution)/shard_map/ppermute | solution.py:23
  67.1 1.5 copy.35
  68.6 14.8 %collective-permute-done.9.rest_2_ = bf16[512,1024]{1,0:T(8,128)(2,1)S(1)} collective-permute-done((bf16[512,1024]{1,0:T(8,128)(2,1)}, bf16[512,1024]{1,0:T(8,128)(2,1)S(1)}, u32[]{:S(2)}, u32[]{:S(2)}) %collective-permute-start.9) | collective-permute-done | bytes 1048608 | tf_op jit(solution)/shard_map/ppermute | solution.py:23
  83.4 1.7 broadcast_select_fusion
  85.2 46.5 %pairs.2 = (bf16[512,1024]{1,0:T(8,128)(2,1)}, bf16[512,1024]{1,0:T(8,128)(2,1)}, bf16[512,1024]{1,0:T(8,128)(2,1)}, bf16[512,1024]{1,0:T(8,128)(2,1)}, bf16[512...) custom-call(f32[4]{0:T(128)} %get-tuple-element.64.gamma_ref, ...), custom_call_target="tpu_custom_call" | custom-call | flops 52428800000 | bytes 10485760 | tf_op jit(solution)/shard_map/pairs/pallas_call | solution.py:225
  132.3 46.7 %pairs.3 = (bf16[512,1024]{1,0:T(8,128)(2,1)}, bf16[512,1024]{1,0:T(8,128)(2,1)}, bf16[512,1024]{1,0:T(8,128)(2,1)}, bf16[512,1024]{1,0:T(8,128)(2,1)}, bf16[512...) custom-call(f32[4]{0:T(128)} %get-tuple-element.65.gamma_ref, ...), custom_call_target="tpu_custom_call" | custom-call | flops 52428800000 | bytes 10485760 | tf_op jit(solution)/shard_map/pairs/pallas_call | solution.py:225
  179.1 1.4 fusion.5
  180.5 1.7 collective-permute-start.14
  182.3 1.4 fusion.10
  189.0 17.8 %collective-permute-done.14 = bf16[512,1024]{1,0:T(8,128)(2,1)} collective-permute-done((bf16[512,1024]{1,0:T(8,128)(2,1)}, bf16[512,1024]{1,0:T(8,128)(2,1)}, u32[]{:S(2)}, u32[]{:S(2)}) %collective-permute-start.14) | collective-permute-done | bytes 1048608 | tf_op jit(solution)/shard_map/ppermute | solution.py:23
  206.9 3.0 %fusion.3 = bf16[512,1024]{1,0:T(8,128)(2,1)} fusion(bf16[512,1024]{1,0:T(8,128)(2,1)S(1)} %collective-permute-done.13, bf16[512,1024]{1,0:T(8,128)(2,1)} %collective-permute-done.14, bf16[512,1024]{1,0:T(8,128)(2,1)S(1)} %copy-done.3, pred[]{:T(512)S(6)} %eq.14), kind=kLoop, calls=%fused_computation.12 | loop fusion | flops 3670016 | bytes 4194305 | tf_op jit(solution)/shard_map/convert_element_type | solution.py:54
  210.8 18.0 %collective-permute-done.18 = bf16[512,1024]{1,0:T(8,128)(2,1)} collective-permute-done((bf16[512,1024]{1,0:T(8,128)(2,1)}, bf16[512,1024]{1,0:T(8,128)(2,1)}, u32[]{:S(2)}, u32[]{:S(2)}) %collective-permute-start.18) | collective-permute-done | bytes 1048608 | tf_op jit(solution)/shard_map/ppermute | solution.py:23
  228.9 2.0 fusion.8
  231.7 2.8 %collective-permute-start.22 = (f32[3,512]{1,0:T(4,128)S(1)}, f32[3,512]{1,0:T(4,128)S(1)}, u32[]{:S(2)}, u32[]{:S(2)}) collective-permute-start(f32[3,512]{1,0:T(4,128)S(1)} %bitcast_add_fusion), channel_id=1, source_target_pairs={{0,24},{2,26},{4,12},{6,14},{8,0},{10,2},{12,20},{14,22},{16,8},{1... | collective-permute-start | bytes 18440 | tf_op jit(solution)/shard_map/ppermute | solution.py:23
  237.1 2.5 collective-permute-start.23
  240.8 16.1 %collective-permute-done.23 = f32[3,512]{1,0:T(4,128)S(1)} collective-permute-done((f32[3,512]{1,0:T(4,128)S(1)}, f32[3,512]{1,0:T(4,128)S(1)}, u32[]{:S(2)}, u32[]{:S(2)}) %collective-permute-start.23) | collective-permute-done | bytes 6176 | tf_op jit(solution)/shard_map/ppermute | solution.py:23
  256.9 5.6 %psum.7 = f32[3,512]{1,0:T(4,128)} all-reduce(f32[3,512]{1,0:T(4,128)S(1)} %fusion.16), channel_id=1, replica_groups=mesh['slab'=16,'head'=2] {'head'}, use_global_device_ids=true, to_apply=%region_0.1 | all-reduce | flops 1536 | bytes 12288 | tf_op jit(solution)/shard_map/psum | solution.py:325
  262.5 2.6 add_convert_fusion.1
  265.1 2.2 add_convert_fusion
  267.3 1.5 pad_maximum_fusion
  (105 shorter events, 23.4 us)
Async XLA Ops:
  2.0 40.6 %collective-permute-start = (f32[4,512]{1,0:T(4,128)S(1)}, f32[4,512]{1,0:T(4,128)S(1)}, u32[]{:S(2)}, u32[]{:S(2)}) collective-permute-start(f32[4,512]{1,0:T(4,128)S(1)} %get-tuple-element.45), channel_id=1, source_target_pairs={{0,4},{2,6},{4,0},{6,2},{8,12},{10,14},{12,8},{14,10},{16,20},{18,... | collective-permute-start | bytes 24584 | tf_op jit(solution)/shard_map/ppermute | solution.py:23
  5.0 58.4 %collective-permute-start.2 = (f32[4,512]{1,0:T(4,128)S(1)}, f32[4,512]{1,0:T(4,128)S(1)}, u32[]{:S(2)}, u32[]{:S(2)}) collective-permute-start(f32[4,512]{1,0:T(4,128)S(1)} %get-tuple-element.45), channel_id=1, source_target_pairs={{0,2},{2,0},{4,6},{6,4},{8,10},{10,8},{12,14},{14,12},{16,18},{18,... | collective-permute-start | bytes 24584 | tf_op jit(solution)/shard_map/ppermute | solution.py:23
  8.1 26.3 %collective-permute-start.4 = (bf16[512,1024]{1,0:T(8,128)(2,1)}, bf16[512,1024]{1,0:T(8,128)(2,1)}, u32[]{:S(2)}, u32[]{:S(2)}) collective-permute-start(bf16[512,1024]{1,0:T(8,128)(2,1)} %get-tuple-element.46.rest_0_), channel_id=1, source_target_pairs={{0,4},{2,6},{4,0},{6,2},{8,12},{10,14},{12,8},{14,10},{16,20},{18,... | collective-permute-start | bytes 3145736 | tf_op jit(solution)/shard_map/ppermute | solution.py:23
  8.1 77.0 %collective-permute-start.6 = (bf16[512,1024]{1,0:T(8,128)(2,1)}, bf16[512,1024]{1,0:T(8,128)(2,1)}, u32[]{:S(2)}, u32[]{:S(2)}) collective-permute-start(bf16[512,1024]{1,0:T(8,128)(2,1)} %get-tuple-element.46.rest_0_), channel_id=1, source_target_pairs={{0,2},{2,0},{4,6},{6,4},{8,10},{10,8},{12,14},{14,12},{16,18},{18,... | collective-permute-start | bytes 3145736 | tf_op jit(solution)/shard_map/ppermute | solution.py:23
  8.6 47.8 %collective-permute-start.8 = (bf16[512,1024]{1,0:T(8,128)(2,1)}, bf16[512,1024]{1,0:T(8,128)(2,1)}, u32[]{:S(2)}, u32[]{:S(2)}) collective-permute-start(bf16[512,1024]{1,0:T(8,128)(2,1)} %get-tuple-element.47.rest_0_), channel_id=1, source_target_pairs={{0,4},{2,6},{4,0},{6,2},{8,12},{10,14},{12,8},{14,10},{16,20},{18,... | collective-permute-start | bytes 3145736 | tf_op jit(solution)/shard_map/ppermute | solution.py:23
  16.6 19.6 %copy-start.19 = (f32[4]{0:T(128)S(1)}, f32[4]{0:T(128)}, u32[]{:S(2)}) copy-start(f32[4]{0:T(128)} %constant.55.clone) | copy-start | bytes 52
  34.4 26.5 %collective-permute-start.5 = (bf16[512,1024]{1,0:T(8,128)(2,1)}, bf16[512,1024]{1,0:T(8,128)(2,1)S(1)}, u32[]{:S(2)}, u32[]{:S(2)}) collective-permute-start(bf16[512,1024]{1,0:T(8,128)(2,1)} %collective-permute-done.4.rest_1_), channel_id=1, source_target_pairs={{0,8},{2,10},{4,28},{6,30},{8,16},{10,18},{12,4},{14,6},{16,24},{1... | collective-permute-start | bytes 3145736 | tf_op jit(solution)/shard_map/ppermute | solution.py:23
  42.6 20.2 %collective-permute-start.1 = (f32[4,512]{1,0:T(4,128)S(1)}, f32[4,512]{1,0:T(4,128)S(1)}, u32[]{:S(2)}, u32[]{:S(2)}) collective-permute-start(f32[4,512]{1,0:T(4,128)S(1)} %collective-permute-done), channel_id=1, source_target_pairs={{0,8},{2,10},{4,28},{6,30},{8,16},{10,18},{12,4},{14,6},{16,24},{1... | collective-permute-start | bytes 24584 | tf_op jit(solution)/shard_map/ppermute | solution.py:23
  56.4 27.0 %collective-permute-start.9 = (bf16[512,1024]{1,0:T(8,128)(2,1)}, bf16[512,1024]{1,0:T(8,128)(2,1)S(1)}, u32[]{:S(2)}, u32[]{:S(2)}) collective-permute-start(bf16[512,1024]{1,0:T(8,128)(2,1)} %collective-permute-done.8.rest_1_), channel_id=1, source_target_pairs={{0,8},{2,10},{4,28},{6,30},{8,16},{10,18},{12,4},{14,6},{16,24},{1... | collective-permute-start | bytes 3145736 | tf_op jit(solution)/shard_map/ppermute | solution.py:23
  62.6 22.6 %collective-permute-start.7 = (bf16[512,1024]{1,0:T(8,128)(2,1)S(1)}, bf16[512,1024]{1,0:T(8,128)(2,1)}, u32[]{:S(2)}, u32[]{:S(2)}) collective-permute-start(bf16[512,1024]{1,0:T(8,128)(2,1)S(1)} %broadcast_select_fusion.1), channel_id=1, source_target_pairs={{0,2},{2,0},{4,6},{6,4},{8,10},{10,8},{12,14},{14,12},{16,18},{18,... | collective-permute-start | bytes 3145736 | tf_op jit(solution)/shard_map/ppermute | solution.py:23
  62.8 69.5 %collective-permute-start.10 = (bf16[512,1024]{1,0:T(8,128)(2,1)}, bf16[512,1024]{1,0:T(8,128)(2,1)}, u32[]{:S(2)}, u32[]{:S(2)}) collective-permute-start(bf16[512,1024]{1,0:T(8,128)(2,1)} %get-tuple-element.47.rest_0_), channel_id=1, source_target_pairs={{0,2},{2,0},{4,6},{6,4},{8,10},{10,8},{12,14},{14,12},{16,18},{18,... | collective-permute-start | bytes 3145736 | tf_op jit(solution)/shard_map/ppermute | solution.py:23
  63.4 3.6 %collective-permute-start.3 = (f32[4,512]{1,0:T(4,128)S(1)}, f32[4,512]{1,0:T(4,128)S(1)}, u32[]{:S(2)}, u32[]{:S(2)}) collective-permute-start(f32[4,512]{1,0:T(4,128)S(1)} %get-tuple-element.59), channel_id=1, source_target_pairs={{0,2},{2,0},{4,6},{6,4},{8,10},{10,8},{12,14},{14,12},{16,18},{18,... | collective-permute-start | bytes 24584 | tf_op jit(solution)/shard_map/ppermute | solution.py:23
  83.4 48.4 %copy-start.8 = (bf16[512,1024]{1,0:T(8,128)(2,1)}, bf16[512,1024]{1,0:T(8,128)(2,1)S(1)}, u32[]{:S(2)}) copy-start(bf16[512,1024]{1,0:T(8,128)(2,1)S(1)} %collective-permute-done.9.rest_2_) | copy-start | bytes 3145732
  85.1 47.2 %collective-permute-start.11 = (bf16[512,1024]{1,0:T(8,128)(2,1)S(1)}, bf16[512,1024]{1,0:T(8,128)(2,1)}, u32[]{:S(2)}, u32[]{:S(2)}) collective-permute-start(bf16[512,1024]{1,0:T(8,128)(2,1)S(1)} %broadcast_select_fusion), channel_id=1, source_target_pairs={{0,2},{2,0},{4,6},{6,4},{8,10},{10,8},{12,14},{14,12},{16,18},{18,... | collective-permute-start | bytes 3145736 | tf_op jit(solution)/shard_map/ppermute | solution.py:23
  131.7 47.4 %collective-permute-start.13 = (bf16[512,1024]{1,0:T(8,128)(2,1)}, bf16[512,1024]{1,0:T(8,128)(2,1)S(1)}, u32[]{:S(2)}, u32[]{:S(2)}) collective-permute-start(bf16[512,1024]{1,0:T(8,128)(2,1)} %get-tuple-element.24), channel_id=1, source_target_pairs={{0,2},{2,0},{4,6},{6,4},{8,10},{10,8},{12,14},{14,12},{16,18},{18,... | collective-permute-start | bytes 3145736 | tf_op jit(solution)/shard_map/ppermute | solution.py:23
  132.3 46.8 %copy-start.9 = (bf16[512,1024]{1,0:T(8,128)(2,1)S(1)}, bf16[512,1024]{1,0:T(8,128)(2,1)}, u32[]{:S(2)}) copy-start(bf16[512,1024]{1,0:T(8,128)(2,1)} %get-tuple-element.25) | copy-start | bytes 3145732
  179.0 3.3 %collective-permute-start.17 = (bf16[512,1024]{1,0:T(8,128)(2,1)}, bf16[512,1024]{1,0:T(8,128)(2,1)S(1)}, u32[]{:S(2)}, u32[]{:S(2)}) collective-permute-start(bf16[512,1024]{1,0:T(8,128)(2,1)} %get-tuple-element.29), channel_id=1, source_target_pairs={{0,2},{2,0},{4,6},{6,4},{8,10},{10,8},{12,14},{14,12},{16,18},{18,... | collective-permute-start | bytes 3145736 | tf_op jit(solution)/shard_map/ppermute | solution.py:23
  180.5 26.3 %collective-permute-start.14 = (bf16[512,1024]{1,0:T(8,128)(2,1)}, bf16[512,1024]{1,0:T(8,128)(2,1)}, u32[]{:S(2)}, u32[]{:S(2)}) collective-permute-start(bf16[512,1024]{1,0:T(8,128)(2,1)} %fusion.5), channel_id=1, source_target_pairs={{0,24},{2,26},{4,12},{6,14},{8,0},{10,2},{12,20},{14,22},{16,8},{1... | collective-permute-start | bytes 3145736 | tf_op jit(solution)/shard_map/ppermute | solution.py:23
  183.7 45.2 %collective-permute-start.18 = (bf16[512,1024]{1,0:T(8,128)(2,1)}, bf16[512,1024]{1,0:T(8,128)(2,1)}, u32[]{:S(2)}, u32[]{:S(2)}) collective-permute-start(bf16[512,1024]{1,0:T(8,128)(2,1)} %fusion.10), channel_id=1, source_target_pairs={{0,24},{2,26},{4,12},{6,14},{8,0},{10,2},{12,20},{14,22},{16,8},{1... | collective-permute-start | bytes 3145736 | tf_op jit(solution)/shard_map/ppermute | solution.py:23
  185.2 21.7 %copy-start.3 = (bf16[512,1024]{1,0:T(8,128)(2,1)S(1)}, bf16[512,1024]{1,0:T(8,128)(2,1)}, u32[]{:S(2)}) copy-start(bf16[512,1024]{1,0:T(8,128)(2,1)} %get-tuple-element.23) | copy-start | bytes 3145732
  187.3 44.4 %collective-permute-start.21 = (f32[3,512]{1,0:T(4,128)S(1)}, f32[3,512]{1,0:T(4,128)S(1)}, u32[]{:S(2)}, u32[]{:S(2)}) collective-permute-start(f32[3,512]{1,0:T(4,128)S(1)} %bitcast.44), channel_id=1, source_target_pairs={{0,2},{2,0},{4,6},{6,4},{8,10},{10,8},{12,14},{14,12},{16,18},{18,... | collective-permute-start | bytes 18440 | tf_op jit(solution)/shard_map/ppermute | solution.py:23
  188.4 74.1 %collective-permute-start.12 = (bf16[512,1024]{1,0:T(8,128)(2,1)}, bf16[512,1024]{1,0:T(8,128)(2,1)}, u32[]{:S(2)}, u32[]{:S(2)}) collective-permute-start(bf16[512,1024]{1,0:T(8,128)(2,1)} %get-tuple-element.22), channel_id=1, source_target_pairs={{0,2},{2,0},{4,6},{6,4},{8,10},{10,8},{12,14},{14,12},{16,18},{18,... | collective-permute-start | bytes 3145736 | tf_op jit(solution)/shard_map/ppermute | solution.py:23
  189.0 76.1 %collective-permute-start.16 = (bf16[512,1024]{1,0:T(8,128)(2,1)}, bf16[512,1024]{1,0:T(8,128)(2,1)}, u32[]{:S(2)}, u32[]{:S(2)}) collective-permute-start(bf16[512,1024]{1,0:T(8,128)(2,1)} %get-tuple-element.27), channel_id=1, source_target_pairs={{0,2},{2,0},{4,6},{6,4},{8,10},{10,8},{12,14},{14,12},{16,18},{18,... | collective-permute-start | bytes 3145736 | tf_op jit(solution)/shard_map/ppermute | solution.py:23
  206.9 22.0 %copy-start.4 = (bf16[512,1024]{1,0:T(8,128)(2,1)S(1)}, bf16[512,1024]{1,0:T(8,128)(2,1)}, u32[]{:S(2)}) copy-start(bf16[512,1024]{1,0:T(8,128)(2,1)} %get-tuple-element.28) | copy-start | bytes 3145732
  209.8 52.6 %collective-permute-start.15 = (bf16[512,1024]{1,0:T(8,128)(2,1)}, bf16[512,1024]{1,0:T(8,128)(2,1)}, u32[]{:S(2)}, u32[]{:S(2)}) collective-permute-start(bf16[512,1024]{1,0:T(8,128)(2,1)} %fusion.3), channel_id=1, source_target_pairs={{0,4},{2,6},{4,0},{6,2},{8,12},{10,14},{12,8},{14,10},{16,20},{18,... | collective-permute-start | bytes 3145736 | tf_op jit(solution)/shard_map/ppermute | solution.py:23
  228.8 10.8 %copy-start.13 = (bf16[256,512]{1,0:T(8,128)(2,1)S(1)}, bf16[256,512]{1,0:T(8,128)(2,1)}, u32[]{:S(2)}) copy-start(bf16[256,512]{1,0:T(8,128)(2,1)} %get-tuple-element.19) | copy-start | bytes 786436
  230.8 26.0 %copy-start.16 = (f32[8,512]{1,0:T(8,128)S(1)}, f32[8,512]{1,0:T(8,128)}, u32[]{:S(2)}) copy-start(f32[8,512]{1,0:T(8,128)} %get-tuple-element.31) | copy-start | bytes 49156
  230.9 26.0 %copy-start.17 = (f32[8,512]{1,0:T(8,128)S(1)}, f32[8,512]{1,0:T(8,128)}, u32[]{:S(2)}) copy-start(f32[8,512]{1,0:T(8,128)} %get-tuple-element.32) | copy-start | bytes 49156
  230.9 34.2 %collective-permute-start.19 = (bf16[512,1024]{1,0:T(8,128)(2,1)S(1)}, bf16[512,1024]{1,0:T(8,128)(2,1)}, u32[]{:S(2)}, u32[]{:S(2)}) collective-permute-start(bf16[512,1024]{1,0:T(8,128)(2,1)S(1)} %fusion.8), channel_id=1, source_target_pairs={{0,4},{2,6},{4,0},{6,2},{8,12},{10,14},{12,8},{14,10},{16,20},{18,... | collective-permute-start | bytes 3145736 | tf_op jit(solution)/shard_map/ppermute | solution.py:23
  231.7 4.2 %collective-permute-start.22 = (f32[3,512]{1,0:T(4,128)S(1)}, f32[3,512]{1,0:T(4,128)S(1)}, u32[]{:S(2)}, u32[]{:S(2)}) collective-permute-start(f32[3,512]{1,0:T(4,128)S(1)} %bitcast_add_fusion), channel_id=1, source_target_pairs={{0,24},{2,26},{4,12},{6,14},{8,0},{10,2},{12,20},{14,22},{16,8},{1... | collective-permute-start | bytes 18440 | tf_op jit(solution)/shard_map/ppermute | solution.py:23
  235.9 1.2 collective-permute-start.20
  237.1 19.8 %collective-permute-start.23 = (f32[3,512]{1,0:T(4,128)S(1)}, f32[3,512]{1,0:T(4,128)S(1)}, u32[]{:S(2)}, u32[]{:S(2)}) collective-permute-start(f32[3,512]{1,0:T(4,128)S(1)} %fusion.14), channel_id=1, source_target_pairs={{0,4},{2,6},{4,0},{6,2},{8,12},{10,14},{12,8},{14,10},{16,20},{18,... | collective-permute-start | bytes 18440 | tf_op jit(solution)/shard_map/ppermute | solution.py:23
  (12 other events, 57.8 us)
